TPU v7x, 256 devices: a whole 4x4x8 slice. The times are simulated.
256 devices in a mesh: rows: 64 (over x, z, core), sub: 4 (over y).
Axes of the slice: x: 4, y: 4, z: 8, core: 2. Of those that a mesh axis runs over, the one named last changes fastest.
Arguments:
- documents: bfloat16 [524288, 1024], P(('rows', 'sub')), may hold values from -40 to 40
- centroids: bfloat16 [1024, 1024], replicated, may hold values from -5 to 5
- cluster_mass: float32 [1024], replicated, may hold values from 0.00024414062 to 0.00390625
Outputs:
- new_centroids: bfloat16 [1024, 1024], P('sub')
- cluster_duals: float32 [1024], replicated
All inputs are finite; a program needn't handle non-finite values.
Results may differ from a plain program's by a relative error of at most 0.0038.
Values may be sent and summed in bfloat16 or wider, within the bound.
No kernel may reach another device: no remote copies, remote signals or barrier semaphores. Data moves between devices by JAX's collectives and lax.ppermute only.
A program may use at most 64 MiB of HBM per device.

v0:
```python
import math

import jax
import jax.numpy as jnp
from jax import lax
from jax.sharding import PartitionSpec as P

D = 1024
ITERS = 3


TAU = 0.8
TEMP = 4.0


def per_device(documents, centroids, cluster_mass):
    n_rows = lax.axis_size("rows")
    n_sub = lax.axis_size("sub")
    local_docs = documents.shape[0]
    n_clusters = centroids.shape[0]
    scores = lax.dot_general(
        documents, centroids, (((1,), (1,)), ((), ())), preferred_element_type=jnp.float32
    ) * (TEMP / math.sqrt(D))
    loga = -jnp.log(jnp.asarray(local_docs * n_rows * n_sub, jnp.float32))
    duals = jnp.zeros((n_clusters,), jnp.float32)
    for step in range(ITERS):
        lse = jax.nn.logsumexp(scores + duals[None, :], axis=1)
        row_duals = TAU * (loga - lse)
        mass = jnp.exp(row_duals[:, None] + scores)
        column_mass = lax.psum(jnp.sum(mass, axis=0), ("rows", "sub"))
        duals = TAU * (jnp.log(cluster_mass) - jnp.log(column_mass))
    plan = mass.astype(jnp.bfloat16)
    slab = n_clusters // n_sub
    total = lax.psum(
        lax.dot_general(
            plan, documents, (((0,), (0,)), ((), ())), preferred_element_type=jnp.float32
        ),
        "rows",
    )
    own = lax.psum_scatter(total, "sub", scatter_dimension=0, tiled=True)
    own_mass = lax.dynamic_slice_in_dim(column_mass, lax.axis_index("sub") * slab, slab, 0)
    return ((own / own_mass[:, None]).astype(jnp.bfloat16), duals)


def solution(mesh):
    return jax.shard_map(
        per_device,
        mesh=mesh,
        in_specs=(P(("rows", "sub"), None), P(), P()),
        out_specs=(P("sub", None), P()),
        check_vma=False,
    )
```

profile of v0, /device:TPU:1, one launch (start us, length us, event | category | flops | bytes accessed | tf_op | source)
XLA Modules:
  0.0 440.9 jit_solution(15094688845599438168)
XLA Ops:
  7.2 0.0 copy-start
  7.2 0.0 reduce-scatter.2.cloned.1.call-start
  7.2 1.5 copy-done
  8.8 6.4 %fusion.5 = (f32[2048]{0:T(1024)S(1)}, f32[2048,1024]{0,1:T(8,128)S(1)}) fusion(bf16[2048,1024]{1,0:T(8,128)(2,1)} %param.3, bf16[1024,1024]{1,0:T(8,128)(2,1)S(1)} %copy-done), kind=kOutput, calls=%fused_computation.23 | convolution fusion | flops 4299159552 | bytes 14688256 | tf_op jit(solution)/shard_map/dot_general | solution.py:21
  15.1 0.0 copy-start.1
  15.2 0.0 copy-start.3
  15.2 1.2 exponential_reduce_fusion.4
  16.4 2.0 copy-done.1
  18.4 1.2 exponential_reduce_fusion.3
  19.5 81.4 %psum.28 = f32[1024]{0:T(1024)S(1)} all-reduce(f32[1024]{0:T(1024)S(1)} %exponential_reduce_fusion.3), channel_id=1, replica_groups=mesh['rows'=64,'sub'=4] {'rows','sub'}, use_global_device_ids=true, to_apply=%region_3.0 | all-reduce | flops 1024 | bytes 8192 | tf_op jit(solution)/shard_map/psum | solution.py:30
  100.9 0.0 copy-done.3
  100.9 0.0 copy-start.2
  101.0 4.2 add_reduce_fusion.1
  105.1 1.6 copy-done.2
  106.7 1.8 exponential_reduce_fusion.2
  108.5 1.2 exponential_reduce_fusion.1
  109.7 72.5 %psum.29 = f32[1024]{0:T(1024)S(1)} all-reduce(f32[1024]{0:T(1024)S(1)} %exponential_reduce_fusion.1), channel_id=1, replica_groups=mesh['rows'=64,'sub'=4] {'rows','sub'}, use_global_device_ids=true, to_apply=%region_7.0 | all-reduce | flops 1024 | bytes 8192 | tf_op jit(solution)/shard_map/psum | solution.py:30
  182.3 0.0 slice-start
  182.3 0.0 copy-start.4
  182.3 4.2 add_reduce_fusion
  186.5 0.0 slice-start.1
  186.5 4.9 %exponential_reduce_fusion = f32[2048]{0:T(1024)S(1)} fusion(f32[2048,1024]{0,1:T(8,128)} %copy-done.1, f32[2048]{0:T(1024)S(1)} %is-finite_select_fusion, f32[1024]{0:T(1024)S(1)} %subtract_multiply_fusion.4), kind=kLoop, calls=%fused_computation.1 | loop fusion | flops 6289408 | bytes 8409088 | tf_op jit(solution)/shard_map/reduce_sum | solution.py:27
  191.5 0.0 slice-done
  191.5 0.0 copy-done.4
  191.5 0.5 slice-done.1
  192.0 6.1 %fusion.2 = f32[1024,1024]{1,0:T(8,128)} fusion(bf16[2048,1024]{1,0:T(8,128)(2,1)S(1)} %copy-done.4, f32[2048,1024]{0,1:T(8,128)S(1)} %bitcast.4, f32[2048]{0:T(1024)S(1)} %subtract_multiply_fusion), kind=kOutput, calls=%fused_computation.11 | convolution fusion | flops 4299161600 | bytes 16785408 | tf_op jit(solution)/shard_map/dot_general | solution.py:35
  198.1 0.0 reduce-scatter.2.cloned.1.call-update
  198.2 0.0 all-reduce.2.cloned.1.call-start
  198.2 45.1 %reduce-scatter.2.cloned.1.call-done = f32[256,1024]{1,0:T(8,128)} async-done(((f32[1024,1024]{1,0:T(8,128)}), f32[256,1024]{1,0:T(8,128)}) %reduce-scatter.2.cloned.1.call-update) | async-done | bytes 1048592 | tf_op jit(solution)/shard_map/reduce_scatter | solution.py:40
  243.3 0.0 all-reduce.2.cloned.1.call-update
  243.3 4.6 %fusion = f32[1024]{0:T(1024)S(1)} fusion(f32[2048,1024]{0,1:T(8,128)} %copy-done.1, f32[2048]{0:T(1024)S(1)} %subtract_multiply_fusion), kind=kLoop, calls=%fused_computation.8 | loop fusion | flops 4193280 | bytes 8400896 | tf_op jit(solution)/shard_map/reduce_sum | solution.py:30
  247.9 76.5 %psum.31 = f32[1024]{0:T(1024)S(1)} all-reduce(f32[1024]{0:T(1024)S(1)} %fusion), channel_id=1, replica_groups=mesh['rows'=64,'sub'=4] {'rows','sub'}, use_global_device_ids=true, to_apply=%region_13.0 | all-reduce | flops 1024 | bytes 8192 | tf_op jit(solution)/shard_map/psum | solution.py:30
  324.4 0.1 dynamic_slice.3
  324.4 0.6 subtract_multiply_fusion.3
  325.0 106.9 %all-reduce.2.cloned.1.call-done = f32[256,1024]{1,0:T(8,128)} async-done(((f32[256,1024]{1,0:T(8,128)}), f32[256,1024]{1,0:T(8,128)}) %all-reduce.2.cloned.1.call-update) | async-done | bytes 1048592 | tf_op jit(solution)/shard_map/psum | solution.py:34
  431.9 2.2 divide_convert_fusion
  (9 shorter events, 0.1 us)
Async XLA Ops:
  7.2 1.6 copy-start
  7.2 236.1 %reduce-scatter.2.cloned.1.call-start = ((), (), s32[]{:S(2)}) async-start(), calls=%async_computation.1 | async-start | bytes 5242880 | tf_op jit(solution)/shard_map/reduce_scatter | solution.py:40
  15.1 3.2 copy-start.1
  15.2 85.8 %copy-start.3 = (f32[1024]{0:T(1024)S(1)}, f32[1024]{0:T(1024)}, u32[]{:S(2)}) copy-start(f32[1024]{0:T(1024)} %param.5) | copy-start | bytes 12292
  100.9 5.8 %copy-start.2 = (f32[2048,1024]{0,1:T(8,128)S(1)}, f32[2048,1024]{0,1:T(8,128)}, u32[]{:S(2)}) copy-start(f32[2048,1024]{0,1:T(8,128)} %copy-done.1) | copy-start | bytes 25165828
  182.3 9.2 %slice-start = ((s8[8388608]{0:T(1024)(128)(4,1)}), s8[4194304]{0:T(1024)(128)(4,1)S(1)}, s32[]{:S(2)}) async-start(s8[8388608]{0:T(1024)(128)(4,1)} %bitcast.3), calls=%async_computation.3 | async-start | bytes 8388608
  182.3 9.2 %copy-start.4 = (bf16[2048,1024]{1,0:T(8,128)(2,1)S(1)}, bf16[2048,1024]{1,0:T(8,128)(2,1)}, u32[]{:S(2)}) copy-start(bf16[2048,1024]{1,0:T(8,128)(2,1)} %param.3) | copy-start | bytes 12582916
  186.5 5.5 %slice-start.1 = ((s8[8388608]{0:T(1024)(128)(4,1)}), s8[4194304]{0:T(1024)(128)(4,1)S(1)}, s32[]{:S(2)}) async-start(s8[8388608]{0:T(1024)(128)(4,1)} %bitcast.3), calls=%async_computation.4 | async-start | bytes 8388608
  198.2 233.8 %all-reduce.2.cloned.1.call-start = ((), (), s32[]{:S(2)}) async-start(), calls=%async_computation.2 | async-start | bytes 2097152 | tf_op jit(solution)/shard_map/psum | solution.py:34
Sparse Core Ops, SparseCore 0:
  198.3 44.9 reduce-scatter.1
  246.7 185.1 all-reduce.1
where the time goes:
time: 443 us; the launch traced here: 441 us
  blocking collectives  230 us (52%)
  waiting for transfers between devices  152 us (34%)
  other arithmetic  26 us (6%)
  between operations  14.2 us (3%)
  matrix products  12.5 us (3%)
  local copies, waits for them, and re-layouts  5.75 us (1%)
    psum x3, blocking collectives, per_device(): column_mass = lax.psum(jnp.sum(mass, axis=0), ('rows', 'sub'))  230 us
    psum x1, waiting for transfers between devices, per_device(): lax.psum(lax.dot_general(plan, documents, (((0,), (0,)), ((), ())), prefe...  107 us
    reduce_scatter x1, waiting for transfers between devices, per_device(): own = lax.psum_scatter(total, 'sub', scatter_dimension=0, tiled=True)  45.1 us
  transfers between devices with their start and end apart: 2, of which 2 were waited for; matrix products, arithmetic and copies ran while one was open for 1% of the time, Pallas kernels for 0%

commit v1 on v0

v1 whole, which is shorter than its diff:
```python
import math

import jax
import jax.numpy as jnp
from jax import lax
from jax.sharding import Mesh
from jax.sharding import PartitionSpec as P

D = 1024
ITERS = 3
TAU = 0.8
TEMP = 4.0
NX, NZ, NC, NY = 4, 8, 2, 4
AXES = ("x", "z", "c", "y")
LANES = 128


def swap_cores(value):
    return lax.ppermute(value, "c", [(0, 1), (1, 0)])


def broadcast_to_group(value, axes, size):
    return lax.all_to_all(jnp.broadcast_to(value[None], (size, *value.shape)), axes, 0, 0, tiled=True)


def sum_all(value):
    value = value + swap_cores(value)
    value = jnp.sum(broadcast_to_group(value, ("x", "y"), NX * NY), axis=0)
    return jnp.sum(broadcast_to_group(value, ("z",), NZ), axis=0)


def split_bf16(value):
    high = lax.reduce_precision(value, 8, 7)
    rest = value - high
    middle = lax.reduce_precision(rest, 8, 7)
    low = rest - middle
    return [piece.astype(jnp.bfloat16) for piece in (high, middle, low)]


def per_device(documents, centroids, cluster_mass):
    n_docs = documents.shape[0] * NX * NZ * NC * NY
    n_clusters = centroids.shape[0]
    half = documents.shape[1] // NC
    core = lax.axis_index("c")
    scores = lax.dot_general(
        documents, centroids, (((1,), (1,)), ((), ())), preferred_element_type=jnp.float32
    ) * (TEMP / math.sqrt(D))
    loga = -jnp.log(jnp.asarray(n_docs, jnp.float32))
    duals = jnp.zeros((n_clusters,), jnp.float32)
    for step in range(ITERS):
        lse = jax.nn.logsumexp(scores + duals[None, :], axis=1)
        row_duals = TAU * (loga - lse)
        mass = jnp.exp(row_duals[:, None] + scores)
        local_mass = jnp.sum(mass, axis=0).reshape(n_clusters // LANES, LANES)
        if step < ITERS - 1:
            column_mass = sum_all(local_mass).reshape(n_clusters)
            duals = TAU * (jnp.log(cluster_mass) - jnp.log(column_mass))
    plan = mass.astype(jnp.bfloat16)
    partial = lax.dot_general(
        plan, documents, (((0,), (0,)), ((), ())), preferred_element_type=jnp.float32
    )
    own = lax.dynamic_slice_in_dim(partial, core * half, half, 1)
    other = lax.dynamic_slice_in_dim(partial, (1 - core) * half, half, 1)
    local_mass = local_mass + swap_cores(local_mass)
    chip = own + swap_cores(other.astype(jnp.bfloat16)).astype(jnp.float32)
    slab = n_clusters // (NX * NY)
    pieces = [piece.reshape(1, n_clusters // half, half) for piece in split_bf16(local_mass)]
    pieces.append(jnp.zeros((1, 2, half), jnp.bfloat16))
    extra = jnp.broadcast_to(jnp.concatenate(pieces, axis=1), (NX * NY, 8, half))
    packed = jnp.concatenate([chip.astype(jnp.bfloat16).reshape(NX * NY, slab, half), extra], axis=1)
    got = lax.all_to_all(packed, ("y", "x"), 0, 0, tiled=True).astype(jnp.float32)
    slab_sum = jnp.sum(got[:, :slab], axis=0)
    mass_xy = jnp.sum(got[:, slab : slab + 2] + got[:, slab + 2 : slab + 4] + got[:, slab + 4 : slab + 6], axis=0)
    rows = slab // NZ
    packed = jnp.concatenate(
        [slab_sum.reshape(NZ, rows, half), jnp.broadcast_to(jnp.pad(mass_xy, ((0, 6), (0, 0)))[None], (NZ, 8, half))],
        axis=1,
    )
    got = lax.all_to_all(packed, ("z",), 0, 0, tiled=True)
    total = jnp.sum(got, axis=0)
    column_mass = total[rows : rows + 2].reshape(n_clusters)
    duals = TAU * (jnp.log(cluster_mass) - jnp.log(column_mass))
    first = (lax.axis_index("y") * NX + lax.axis_index("x")) * slab + lax.axis_index("z") * rows
    own_mass = lax.dynamic_slice_in_dim(column_mass, first, rows, 0)
    mine = (total[:rows] / own_mass[:, None]).astype(jnp.bfloat16)
    block = broadcast_to_group(mine, ("x", "z"), NX * NZ).reshape(n_clusters // NY, half)
    other = swap_cores(block)
    left = jnp.where(core == 0, block, other)
    right = jnp.where(core == 0, other, block)
    return jnp.concatenate([left, right], axis=1), duals


def solution(mesh):
    grid = Mesh(mesh.devices.reshape(NX, NZ, NC, NY), AXES)
    return jax.shard_map(
        per_device,
        mesh=grid,
        in_specs=(P(AXES, None), P(), P()),
        out_specs=(P("y", None), P()),
        check_vma=False,
    )
```

time: 443 us -> 156 us (0.35)
  blocking collectives: 230 us -> 69.6 us
  waiting for transfers between devices: 152 us -> 20 us
  starting transfers between devices: 0.08 us -> 20.4 us
  between operations: 14.2 us -> 0.96 us
    psum x3 -> x0, blocking collectives: 230 us -> none  [per_device(): column_mass = lax.psum(jnp.sum(mass, axis=0), ('rows', 'sub'))]
    psum x1 -> x0, waiting for transfers between devices: 107 us -> none  [per_device(): lax.psum(lax.dot_general(plan, documents, (((0,), (0,)), ((), ())), prefe...]
    all_to_all x0 -> x5, blocking collectives: none -> 69.6 us  [the longest x4 48.7 us: broadcast_to_group(): lax.all_to_all(jnp.broadcast_to(value[None], (size, *value.shape)), axes,...]
    reduce_scatter x1 -> x0, waiting for transfers between devices: 45.1 us -> none  [per_device(): own = lax.psum_scatter(total, 'sub', scatter_dimension=0, tiled=True)]
    all_to_all x0 -> x2, waiting for transfers between devices: none -> 16.7 us  [the longest x1 10.1 us: per_device(): got = lax.all_to_all(packed, ('z',), 0, 0, tiled=True)]
    ppermute x0 -> x5, starting transfers between devices: none -> 13.5 us  [swap_cores(): return lax.ppermute(value, 'c', [(0, 1), (1, 0)])]
    all_to_all x0 -> x2, starting transfers between devices: none -> 6.93 us  [the longest x1 3.52 us: broadcast_to_group(): lax.all_to_all(jnp.broadcast_to(value[None], (size, *value.shape)), axes,...]
  transfers between devices with their start and end apart: 2 -> 7, of which waited for: 2 -> 6; matrix products, arithmetic and copies ran while one was open for 1% -> 1% of each run, Pallas kernels for 0% -> 0%
where the time goes in v1:
time: 156 us; the launch traced here: 155 us
  blocking collectives  69.6 us (45%)
  other arithmetic  25 us (16%)
  starting transfers between devices  20.4 us (13%)
  waiting for transfers between devices  20 us (13%)
  matrix products  10.9 us (7%)
  local copies, waits for them, and re-layouts  8.45 us (5%)
    all_to_all x4, blocking collectives, broadcast_to_group(): lax.all_to_all(jnp.broadcast_to(value[None], (size, *value.shape)), axes,...  48.7 us
    all_to_all x1, blocking collectives, per_device(): lax.all_to_all(packed, ('y', 'x'), 0, 0, tiled=True).astype(jnp.float32)  21 us
    ppermute x5, starting transfers between devices, swap_cores(): return lax.ppermute(value, 'c', [(0, 1), (1, 0)])  13.5 us
    all_to_all x1, waiting for transfers between devices, per_device(): got = lax.all_to_all(packed, ('z',), 0, 0, tiled=True)  10.1 us
    reduce_max x2, other arithmetic, per_device(): lse = jax.nn.logsumexp(scores + duals[None, :], axis=1)  8.3 us
    reduce_sum x3, other arithmetic, per_device(): lse = jax.nn.logsumexp(scores + duals[None, :], axis=1)  7.95 us
    all_to_all x1, waiting for transfers between devices, broadcast_to_group(): lax.all_to_all(jnp.broadcast_to(value[None], (size, *value.shape)), axes,...  6.59 us
    unnamed x18, local copies, waits for them, and re-layouts  6.43 us
  transfers between devices with their start and end apart: 7, of which 6 were waited for; matrix products, arithmetic and copies ran while one was open for 1% of the time, Pallas kernels for 0%

profile of v1, /device:TPU:1, one launch (start us, length us, event | category | flops | bytes accessed | tf_op | source)
XLA Modules:
  0.0 155.3 jit_solution(13891694823323656533)
XLA Ops:
  0.6 0.0 copy-start
  0.6 1.6 %copy-done = bf16[1024,1024]{1,0:T(8,128)(2,1)S(1)} copy-done((bf16[1024,1024]{1,0:T(8,128)(2,1)S(1)}, bf16[1024,1024]{1,0:T(8,128)(2,1)}, u32[]{:S(2)}) %copy-start) | copy-done | bytes 2097176
  2.2 6.4 %fusion.10 = (f32[2048]{0:T(1024)S(1)}, f32[2048,1024]{0,1:T(8,128)S(1)}) fusion(bf16[2048,1024]{1,0:T(8,128)(2,1)} %param.3, bf16[1024,1024]{1,0:T(8,128)(2,1)S(1)} %copy-done), kind=kOutput, calls=%fused_computation.47 | convolution fusion | flops 4299159552 | bytes 14688256 | tf_op jit(solution)/shard_map/dot_general | solution.py:45
  8.6 1.2 exponential_reduce_fusion.4
  9.8 1.2 exponential_reduce_fusion.3
  11.0 0.8 copy-done.1
  11.8 3.2 %collective-permute-start = (f32[8,128]{1,0:T(8,128)S(1)}, f32[8,128]{1,0:T(8,128)S(1)}, u32[]{:S(2)}, u32[]{:S(2)}) collective-permute-start(f32[8,128]{1,0:T(8,128)S(1)} %bitcast.39), channel_id=1, source_target_pairs={{0,4},{4,0},{1,5},{5,1},{2,6},{6,2},{3,7},{7,3},{8,12},{12,8},{9,1... | collective-permute-start | bytes 12296 | tf_op jit(solution)/shard_map/ppermute | solution.py:19
  15.0 0.8 collective-permute-done
  15.9 11.4 %all_to_all.35 = f32[16,8,128]{2,1,0:T(8,128)S(1)} all-to-all(f32[16,8,128]{2,1,0:T(8,128)S(1)} %broadcast_in_dim.18), channel_id=1, replica_groups=mesh['x'=4,'z'=8,'c'=2,'y'=4] {'x','y'}, dimensions={0} | all-to-all | bytes 131072 | tf_op jit(solution)/shard_map/all_to_all | solution.py:23
  27.3 14.9 %all_to_all.36 = f32[8,8,128]{2,1,0:T(8,128)S(1)} all-to-all(f32[8,8,128]{2,1,0:T(8,128)S(1)} %broadcast_in_dim.19), channel_id=1, replica_groups=mesh['x'=4,'z'=8,'c'=2,'y'=4] {'z'}, dimensions={0} | all-to-all | bytes 65536 | tf_op jit(solution)/shard_map/all_to_all | solution.py:23
  42.2 4.2 %add_reduce_fusion.1 = f32[2048]{0:T(1024)S(1)} fusion(f32[2048,1024]{0,1:T(8,128)} %copy-done.1, f32[1024]{0:T(1024)S(1)} %fusion.9), kind=kLoop, calls=%fused_computation.7 | loop fusion | flops 4192256 | bytes 8400896 | tf_op jit(solution)/shard_map/reduce_max | solution.py:51
  46.3 1.6 %copy-done.2 = f32[2048,1024]{0,1:T(8,128)S(1)} copy-done((f32[2048,1024]{0,1:T(8,128)S(1)}, f32[2048,1024]{0,1:T(8,128)}, u32[]{:S(2)}) %copy-start.2) | copy-done | bytes 8388632
  47.9 1.8 %exponential_reduce_fusion.2 = f32[2048]{0:T(1024)S(1)} fusion(f32[2048,1024]{0,1:T(8,128)S(1)} %copy-done.2, f32[2048]{0:T(1024)S(1)} %is-finite_select_fusion.1, f32[1024]{0:T(1024)S(1)} %fusion.9), kind=kLoop, calls=%fused_computation.3 | loop fusion | flops 6289408 | bytes 8409088 | tf_op jit(solution)/shard_map/reduce_sum | solution.py:51
  49.7 1.2 exponential_reduce_fusion.1
  50.9 3.3 %collective-permute-start.1 = (f32[8,128]{1,0:T(8,128)S(1)}, f32[8,128]{1,0:T(8,128)S(1)}, u32[]{:S(2)}, u32[]{:S(2)}) collective-permute-start(f32[8,128]{1,0:T(8,128)S(1)} %bitcast.40), channel_id=1, source_target_pairs={{0,4},{4,0},{1,5},{5,1},{2,6},{6,2},{3,7},{7,3},{8,12},{12,8},{9,1... | collective-permute-start | bytes 12296 | tf_op jit(solution)/shard_map/ppermute | solution.py:19
  54.2 0.8 collective-permute-done.1
  55.1 9.5 %all_to_all.37 = f32[16,8,128]{2,1,0:T(8,128)S(1)} all-to-all(f32[16,8,128]{2,1,0:T(8,128)S(1)} %broadcast_in_dim.20), channel_id=1, replica_groups=mesh['x'=4,'z'=8,'c'=2,'y'=4] {'x','y'}, dimensions={0} | all-to-all | bytes 131072 | tf_op jit(solution)/shard_map/all_to_all | solution.py:23
  64.5 0.6 broadcast_in_dim.21
  65.2 3.5 %all-to-all-start.3 = ((f32[8,8,128]{2,1,0:T(8,128)}), f32[8,8,128]{2,1,0:T(8,128)S(1)}, u32[]{:S(2)}, u32[]{:S(2)}) async-start(f32[8,8,128]{2,1,0:T(8,128)} %broadcast_in_dim.21), calls=%async_computation.3 | async-start | bytes 65536 | tf_op jit(solution)/shard_map/all_to_all | solution.py:23
  68.7 6.6 %all-to-all-done.3 = f32[8,8,128]{2,1,0:T(8,128)S(1)} async-done(((f32[8,8,128]{2,1,0:T(8,128)}), f32[8,8,128]{2,1,0:T(8,128)S(1)}, u32[]{:S(2)}, u32[]{:S(2)}) %all-to-all-start.3) | async-done | bytes 32800 | tf_op jit(solution)/shard_map/all_to_all | solution.py:23
  75.3 4.2 %add_reduce_fusion = f32[2048]{0:T(1024)S(1)} fusion(f32[2048,1024]{0,1:T(8,128)} %copy-done.1, f32[1024]{0:T(1024)S(1)} %fusion.8), kind=kLoop, calls=%fused_computation.6 | loop fusion | flops 4192256 | bytes 8400896 | tf_op jit(solution)/shard_map/reduce_max | solution.py:51
  79.5 5.0 %exponential_reduce_fusion = f32[2048]{0:T(1024)S(1)} fusion(f32[2048,1024]{0,1:T(8,128)} %copy-done.1, f32[2048]{0:T(1024)S(1)} %is-finite_select_fusion, f32[1024]{0:T(1024)S(1)} %fusion.8), kind=kLoop, calls=%fused_computation.1 | loop fusion | flops 6289408 | bytes 8409088 | tf_op jit(solution)/shard_map/reduce_sum | solution.py:51
  84.5 0.5 slice-done.1
  85.0 4.5 %fusion.2 = f32[1024,1024]{1,0:T(8,128)S(1)} fusion(bf16[2048,1024]{1,0:T(8,128)(2,1)S(1)} %copy-done.5, f32[2048,1024]{0,1:T(8,128)S(1)} %bitcast.34, f32[2048]{0:T(1024)S(1)} %subtract_multiply_fusion), kind=kOutput, calls=%fused_computation.11 | convolution fusion | flops 4299161600 | bytes 16785408 | tf_op jit(solution)/shard_map/dot_general | solution.py:59
  89.6 1.9 %copy-done.3 = f32[1024,1024]{1,0:T(8,128)} copy-done((f32[1024,1024]{1,0:T(8,128)}, f32[1024,1024]{1,0:T(8,128)S(1)}, u32[]{:S(2)}) %copy-start.3) | copy-done | bytes 4194328
  91.5 1.1 dynamic-slice_convert_fusion
  92.6 2.9 %collective-permute-start.2 = (bf16[1024,512]{1,0:T(8,128)(2,1)}, bf16[1024,512]{1,0:T(8,128)(2,1)S(1)}, u32[]{:S(2)}, u32[]{:S(2)}) collective-permute-start(bf16[1024,512]{1,0:T(8,128)(2,1)} %dynamic-slice_convert_fusion), channel_id=1, source_target_pairs={{0,4},{4,0},{1,5},{5,1},{2,6},{6,2},{3,7},{7,3},{8,12},{12,8},{9,1... | collective-permute-start | bytes 3145736 | tf_op jit(solution)/shard_map/ppermute | solution.py:19
  95.5 1.2 fusion
  96.7 0.1 collective-permute-start.3
  96.8 0.1 pad.14.clone
  96.9 1.1 collective-permute-done.3
  98.1 0.1 maximum_bitcast_fusion
  98.2 1.9 %add_convert_fusion = bf16[1024,512]{1,0:T(8,128)(2,1)S(1)} fusion(bf16[1024,512]{1,0:T(8,128)(2,1)S(1)} %collective-permute-done.2, f32[1024,1024]{1,0:T(8,128)} %copy-done.3, s32[]{:T(128)S(6)} %select_n.55), kind=kLoop, calls=%fused_computation.14 | loop fusion | flops 1572864 | bytes 4194308 | tf_op jit(solution)/shard_map/convert_element_type | solution.py:70
  100.1 0.1 pad_maximum_fusion
  100.2 21.0 %all_to_all.38 = bf16[16,72,512]{2,1,0:T(8,128)(2,1)S(1)} all-to-all(bf16[16,72,512]{2,1,0:T(8,128)(2,1)S(1)} %pad_maximum_fusion), channel_id=1, replica_groups=mesh['x'=4,'z'=8,'c'=2,'y'=4] {'y','x'}, dimensions={0} | all-to-all | bytes 2359296 | tf_op jit(solution)/shard_map/all_to_all | solution.py:71
  121.2 0.3 convert_element_type.36
  121.5 0.1 fusion.5
  121.6 0.2 slice_reduce_fusion
  121.8 0.7 pad_maximum_fusion.2
  122.6 3.4 %all-to-all-start.5 = ((f32[8,16,512]{2,1,0:T(8,128)}), f32[8,16,512]{2,1,0:T(8,128)S(1)}, u32[]{:S(2)}, u32[]{:S(2)}) async-start(f32[8,16,512]{2,1,0:T(8,128)} %pad_maximum_fusion.2), calls=%async_computation.5 | async-start | bytes 524288 | tf_op jit(solution)/shard_map/all_to_all | solution.py:79
  126.0 10.1 %all-to-all-done.5 = f32[8,16,512]{2,1,0:T(8,128)S(1)} async-done(((f32[8,16,512]{2,1,0:T(8,128)}), f32[8,16,512]{2,1,0:T(8,128)S(1)}, u32[]{:S(2)}, u32[]{:S(2)}) %all-to-all-start.5) | async-done | bytes 262176 | tf_op jit(solution)/shard_map/all_to_all | solution.py:79
  136.2 0.1 dynamic_slice.11
  136.2 0.1 fusion.6
  136.3 13.0 %all_to_all.39 = bf16[32,8,512]{2,1,0:T(8,128)(2,1)S(1)} all-to-all(bf16[32,8,512]{2,1,0:T(8,128)(2,1)S(1)} %broadcast_in_dim.26), channel_id=1, replica_groups=mesh['x'=4,'z'=8,'c'=2,'y'=4] {'x','z'}, dimensions={0} | all-to-all | bytes 524288 | tf_op jit(solution)/shard_map/all_to_all | solution.py:23
  149.3 3.9 %collective-permute-start.4 = (bf16[256,512]{1,0:T(8,128)(2,1)S(1)}, bf16[256,512]{1,0:T(8,128)(2,1)S(1)}, u32[]{:S(2)}, u32[]{:S(2)}) collective-permute-start(bf16[256,512]{1,0:T(8,128)(2,1)S(1)} %bitcast.36), channel_id=1, source_target_pairs={{0,4},{4,0},{1,5},{5,1},{2,6},{6,2},{3,7},{7,3},{8,12},{12,8},{9,1... | collective-permute-start | bytes 786440 | tf_op jit(solution)/shard_map/ppermute | solution.py:19
  153.3 0.6 subtract_multiply_fusion.3
  153.9 0.6 collective-permute-done.4
  154.5 0.9 pad_maximum_fusion.1
  (42 shorter events, 0.3 us)
Async XLA Ops:
  0.6 1.6 %copy-start = (bf16[1024,1024]{1,0:T(8,128)(2,1)S(1)}, bf16[1024,1024]{1,0:T(8,128)(2,1)}, u32[]{:S(2)}) copy-start(bf16[1024,1024]{1,0:T(8,128)(2,1)} %param.4) | copy-start | bytes 6291460
  8.6 3.2 %copy-start.1 = (f32[2048,1024]{0,1:T(8,128)}, f32[2048,1024]{0,1:T(8,128)S(1)}, u32[]{:S(2)}) copy-start(f32[2048,1024]{0,1:T(8,128)S(1)} %get-tuple-element.8) | copy-start | bytes 25165828
  8.6 33.5 %copy-start.4 = (f32[1024]{0:T(1024)S(1)}, f32[1024]{0:T(1024)}, u32[]{:S(2)}) copy-start(f32[1024]{0:T(1024)} %param.5) | copy-start | bytes 12292
  11.8 4.0 %collective-permute-start = (f32[8,128]{1,0:T(8,128)S(1)}, f32[8,128]{1,0:T(8,128)S(1)}, u32[]{:S(2)}, u32[]{:S(2)}) collective-permute-start(f32[8,128]{1,0:T(8,128)S(1)} %bitcast.39), channel_id=1, source_target_pairs={{0,4},{4,0},{1,5},{5,1},{2,6},{6,2},{3,7},{7,3},{8,12},{12,8},{9,1... | collective-permute-start | bytes 12296 | tf_op jit(solution)/shard_map/ppermute | solution.py:19
  42.1 5.8 %copy-start.2 = (f32[2048,1024]{0,1:T(8,128)S(1)}, f32[2048,1024]{0,1:T(8,128)}, u32[]{:S(2)}) copy-start(f32[2048,1024]{0,1:T(8,128)} %copy-done.1) | copy-start | bytes 25165828
  50.9 4.1 %collective-permute-start.1 = (f32[8,128]{1,0:T(8,128)S(1)}, f32[8,128]{1,0:T(8,128)S(1)}, u32[]{:S(2)}, u32[]{:S(2)}) collective-permute-start(f32[8,128]{1,0:T(8,128)S(1)} %bitcast.40), channel_id=1, source_target_pairs={{0,4},{4,0},{1,5},{5,1},{2,6},{6,2},{3,7},{7,3},{8,12},{12,8},{9,1... | collective-permute-start | bytes 12296 | tf_op jit(solution)/shard_map/ppermute | solution.py:19
  65.2 10.1 %all-to-all-start.3 = ((f32[8,8,128]{2,1,0:T(8,128)}), f32[8,8,128]{2,1,0:T(8,128)S(1)}, u32[]{:S(2)}, u32[]{:S(2)}) async-start(f32[8,8,128]{2,1,0:T(8,128)} %broadcast_in_dim.21), calls=%async_computation.3 | async-start | bytes 65536 | tf_op jit(solution)/shard_map/all_to_all | solution.py:23
  75.3 9.2 %slice-start = ((s8[8388608]{0:T(1024)(128)(4,1)}), s8[4194304]{0:T(1024)(128)(4,1)S(1)}, s32[]{:S(2)}) async-start(s8[8388608]{0:T(1024)(128)(4,1)} %bitcast.33), calls=%async_computation.7 | async-start | bytes 8388608
  75.3 9.2 %copy-start.5 = (bf16[2048,1024]{1,0:T(8,128)(2,1)S(1)}, bf16[2048,1024]{1,0:T(8,128)(2,1)}, u32[]{:S(2)}) copy-start(bf16[2048,1024]{1,0:T(8,128)(2,1)} %param.3) | copy-start | bytes 12582916
  79.5 5.5 %slice-start.1 = ((s8[8388608]{0:T(1024)(128)(4,1)}), s8[4194304]{0:T(1024)(128)(4,1)S(1)}, s32[]{:S(2)}) async-start(s8[8388608]{0:T(1024)(128)(4,1)} %bitcast.33), calls=%async_computation.8 | async-start | bytes 8388608
  89.5 1.9 %copy-start.3 = (f32[1024,1024]{1,0:T(8,128)}, f32[1024,1024]{1,0:T(8,128)S(1)}, u32[]{:S(2)}) copy-start(f32[1024,1024]{1,0:T(8,128)S(1)} %fusion.2) | copy-start | bytes 12582916
  92.6 5.6 %collective-permute-start.2 = (bf16[1024,512]{1,0:T(8,128)(2,1)}, bf16[1024,512]{1,0:T(8,128)(2,1)S(1)}, u32[]{:S(2)}, u32[]{:S(2)}) collective-permute-start(bf16[1024,512]{1,0:T(8,128)(2,1)} %dynamic-slice_convert_fusion), channel_id=1, source_target_pairs={{0,4},{4,0},{1,5},{5,1},{2,6},{6,2},{3,7},{7,3},{8,12},{12,8},{9,1... | collective-permute-start | bytes 3145736 | tf_op jit(solution)/shard_map/ppermute | solution.py:19
  96.7 1.3 collective-permute-start.3
  122.6 13.6 %all-to-all-start.5 = ((f32[8,16,512]{2,1,0:T(8,128)}), f32[8,16,512]{2,1,0:T(8,128)S(1)}, u32[]{:S(2)}, u32[]{:S(2)}) async-start(f32[8,16,512]{2,1,0:T(8,128)} %pad_maximum_fusion.2), calls=%async_computation.5 | async-start | bytes 524288 | tf_op jit(solution)/shard_map/all_to_all | solution.py:79
  149.3 5.1 %collective-permute-start.4 = (bf16[256,512]{1,0:T(8,128)(2,1)S(1)}, bf16[256,512]{1,0:T(8,128)(2,1)S(1)}, u32[]{:S(2)}, u32[]{:S(2)}) collective-permute-start(bf16[256,512]{1,0:T(8,128)(2,1)S(1)} %bitcast.36), channel_id=1, source_target_pairs={{0,4},{4,0},{1,5},{5,1},{2,6},{6,2},{3,7},{7,3},{8,12},{12,8},{9,1... | collective-permute-start | bytes 786440 | tf_op jit(solution)/shard_map/ppermute | solution.py:19

commit v2 on v0

v2 whole, which is shorter than its diff:
```python
import functools
import math

import jax
import jax.numpy as jnp
from jax import lax
from jax.experimental import pallas as pl
from jax.experimental.pallas import tpu as pltpu
from jax.sharding import Mesh
from jax.sharding import PartitionSpec as P

D = 1024
TAU = 0.8
TEMP = 4.0
NX, NZ, NC, NY = 4, 8, 2, 4
AXES = ("x", "z", "c", "y")
LANES = 128
BLOCK = 256
TILE = 256
MIB = 2**20


def swap_cores(value):
    return lax.ppermute(value, "c", [(0, 1), (1, 0)])


def broadcast_to_group(value, axes, size):
    return lax.all_to_all(jnp.broadcast_to(value[None], (size, *value.shape)), axes, 0, 0, tiled=True)


def sum_all(value):
    value = jnp.sum(broadcast_to_group(value, ("x", "y"), NX * NY), axis=0)
    return jnp.sum(broadcast_to_group(value, ("z", "c"), NZ * NC), axis=0)


def masses(scores, duals, loga):
    shifted = scores if duals is None else scores + duals
    top = jnp.max(shifted, axis=0, keepdims=True)
    lse = top + jnp.log(jnp.sum(jnp.exp(shifted - top), axis=0, keepdims=True))
    return jnp.exp(TAU * (loga - lse) + scores)


def first_kernel(loga, n_blocks, docs_ref, cent_ref, scores_ref, mass_ref, held, acc):
    step = pl.program_id(0)

    @pl.when(step == 0)
    def _():
        held[...] = jnp.zeros_like(held)
        acc[...] = jnp.zeros_like(acc)

    before = held[...]
    scores = lax.dot_general(
        cent_ref[...], docs_ref[...], (((1,), (1,)), ((), ())), preferred_element_type=jnp.float32
    ) * (TEMP / math.sqrt(D))
    total = jnp.zeros(acc.shape, jnp.float32)
    for lane in range(0, BLOCK, LANES):
        total += masses(before[:, lane : lane + LANES], None, loga)
    acc[...] += jnp.where(step > 0, total, 0.0)
    scores_ref[...] = scores
    held[...] = scores

    @pl.when(step == n_blocks)
    def _():
        mass_ref[...] = jnp.sum(acc[...].T, axis=0, keepdims=True)


def first_call(documents, centroids, loga):
    n_docs, dim = documents.shape
    n_clusters = centroids.shape[0]
    n_blocks = n_docs // BLOCK
    last = n_blocks - 1
    return pl.pallas_call(
        functools.partial(first_kernel, loga, n_blocks),
        grid=(n_blocks + 1,),
        in_specs=[
            pl.BlockSpec((BLOCK, dim), lambda i: (jnp.minimum(i, last), 0)),
            pl.BlockSpec((n_clusters, dim), lambda i: (0, 0)),
        ],
        out_specs=[
            pl.BlockSpec((n_clusters, BLOCK), lambda i: (0, jnp.minimum(i, last))),
            pl.BlockSpec((1, n_clusters), lambda i: (0, 0)),
        ],
        out_shape=[
            jax.ShapeDtypeStruct((n_clusters, n_docs), jnp.float32),
            jax.ShapeDtypeStruct((1, n_clusters), jnp.float32),
        ],
        scratch_shapes=[
            pltpu.VMEM((n_clusters, BLOCK), jnp.float32),
            pltpu.VMEM((n_clusters, LANES), jnp.float32),
        ],
        compiler_params=pltpu.CompilerParams(vmem_limit_bytes=62 * MIB),
        name="first",
    )(documents, centroids)


def start_duals(duals_ref, duals_col, acc):
    duals_col[...] = jnp.broadcast_to(duals_ref[...], (LANES, duals_ref.shape[1])).T
    acc[...] = jnp.zeros_like(acc)


def middle_kernel(loga, n_blocks, scores_ref, duals_ref, mass_ref, duals_col, acc):
    step = pl.program_id(0)

    @pl.when(step == 0)
    def _():
        start_duals(duals_ref, duals_col, acc)

    duals = duals_col[...]
    total = acc[...]
    for lane in range(0, BLOCK, LANES):
        total += masses(scores_ref[:, lane : lane + LANES], duals, loga)
    acc[...] = total

    @pl.when(step == n_blocks - 1)
    def _():
        mass_ref[...] = jnp.sum(acc[...].T, axis=0, keepdims=True)


def middle_call(scores, duals, loga):
    n_clusters, n_docs = scores.shape
    n_blocks = n_docs // BLOCK
    return pl.pallas_call(
        functools.partial(middle_kernel, loga, n_blocks),
        grid=(n_blocks,),
        in_specs=[
            pl.BlockSpec((n_clusters, BLOCK), lambda i: (0, i)),
            pl.BlockSpec((1, n_clusters), lambda i: (0, 0)),
        ],
        out_specs=pl.BlockSpec((1, n_clusters), lambda i: (0, 0)),
        out_shape=jax.ShapeDtypeStruct((1, n_clusters), jnp.float32),
        scratch_shapes=[
            pltpu.VMEM((n_clusters, LANES), jnp.float32),
            pltpu.VMEM((n_clusters, LANES), jnp.float32),
        ],
        compiler_params=pltpu.CompilerParams(vmem_limit_bytes=62 * MIB),
        name="middle",
    )(scores, duals)


def last_kernel(loga, n_blocks, n_tiles, core_ref, scores_ref, duals_ref, docs_ref, send_ref, own_ref, mass_ref, plan, duals_col, acc):
    step = pl.program_id(0)

    @pl.when(step == 0)
    def _():
        start_duals(duals_ref, duals_col, acc)

    @pl.when(step < n_blocks)
    def _():
        duals = duals_col[...]
        total = acc[...]
        for lane in range(0, BLOCK, LANES):
            mass = masses(scores_ref[:, lane : lane + LANES], duals, loga)
            total += mass
            plan[:, pl.ds(pl.multiple_of(step * BLOCK + lane, LANES), LANES)] = mass.astype(jnp.bfloat16)
        acc[...] = total

    @pl.when(step == n_blocks)
    def _():
        mass_ref[...] = jnp.sum(acc[...].T, axis=0, keepdims=True)

    def tile():
        return lax.dot_general(
            plan[...], docs_ref[...], (((1,), (0,)), ((), ())), preferred_element_type=jnp.float32
        )

    @pl.when(jnp.logical_and(step >= n_blocks, step < n_blocks + n_tiles))
    def _():
        send_ref[...] = tile().astype(jnp.bfloat16)

    @pl.when(step >= n_blocks + n_tiles)
    def _():
        own_ref[...] = tile()


def last_call(scores, duals, documents, core, loga):
    n_clusters, n_docs = scores.shape
    dim = documents.shape[1]
    half = dim // NC
    n_blocks = n_docs // BLOCK
    n_tiles = half // TILE

    def column(i, core):
        tile = jnp.clip(i - n_blocks, 0, 2 * n_tiles - 1)
        return lax.rem(tile + (1 - core[0]) * n_tiles, 2 * n_tiles)

    return pl.pallas_call(
        functools.partial(last_kernel, loga, n_blocks, n_tiles),
        grid_spec=pltpu.PrefetchScalarGridSpec(
            num_scalar_prefetch=1,
            grid=(n_blocks + 2 * n_tiles,),
            in_specs=[
                pl.BlockSpec((n_clusters, BLOCK), lambda i, core: (0, jnp.minimum(i, n_blocks - 1))),
                pl.BlockSpec((1, n_clusters), lambda i, core: (0, 0)),
                pl.BlockSpec((n_docs, TILE), lambda i, core: (0, column(i, core))),
            ],
            out_specs=[
                pl.BlockSpec((n_clusters, TILE), lambda i, core: (0, jnp.clip(i - n_blocks, 0, n_tiles - 1))),
                pl.BlockSpec((n_clusters, TILE), lambda i, core: (0, jnp.clip(i - n_blocks - n_tiles, 0, n_tiles - 1))),
                pl.BlockSpec((1, n_clusters), lambda i, core: (0, 0)),
            ],
            scratch_shapes=[
                pltpu.VMEM((n_clusters, n_docs), jnp.bfloat16),
                pltpu.VMEM((n_clusters, LANES), jnp.float32),
                pltpu.VMEM((n_clusters, LANES), jnp.float32),
            ],
        ),
        out_shape=[
            pltpu.VMEM((n_clusters, half), jnp.bfloat16),
            pltpu.VMEM((n_clusters, half), jnp.float32),
            pltpu.VMEM((1, n_clusters), jnp.float32),
        ],
        compiler_params=pltpu.CompilerParams(vmem_limit_bytes=56 * MIB),
        name="last",
    )(core, scores, duals, documents)


def pack_kernel(per_step, slab, own_ref, got_ref, mass_ref, mass_got_ref, out_ref):
    half = own_ref.shape[1]
    total = own_ref[...] + got_ref[...].astype(jnp.float32)
    out_ref[:, :slab, :] = total.astype(jnp.bfloat16).reshape(per_step, slab, half)
    mass = mass_ref[...] + mass_got_ref[...]
    high = mass.astype(jnp.bfloat16).astype(jnp.float32)
    middle = (mass - high).astype(jnp.bfloat16).astype(jnp.float32)
    low = mass - high - middle
    rows = lax.broadcasted_iota(jnp.int32, (8, half), 0)
    extra = jnp.zeros((8, half), jnp.float32)
    for index, piece in enumerate((high, middle, low)):
        for part in range(2):
            row = jnp.broadcast_to(piece[:, part * half : (part + 1) * half], (8, half))
            extra = jnp.where(rows == 2 * index + part, row, extra)
    extra = extra.astype(jnp.bfloat16)
    for k in range(per_step):
        out_ref[k, slab:, :] = extra


def pack_call(own, got, mass, mass_got):
    n_clusters, half = own.shape
    slab = n_clusters // (NX * NY)
    per_step = 4
    steps = NX * NY // per_step
    return pl.pallas_call(
        functools.partial(pack_kernel, per_step, slab),
        grid=(steps,),
        in_specs=[
            pl.BlockSpec((per_step * slab, half), lambda i: (i, 0)),
            pl.BlockSpec((per_step * slab, half), lambda i: (i, 0)),
            pl.BlockSpec((1, n_clusters), lambda i: (0, 0)),
            pl.BlockSpec((1, n_clusters), lambda i: (0, 0)),
        ],
        out_specs=pl.BlockSpec((per_step, slab + 8, half), lambda i: (i, 0, 0)),
        out_shape=jax.ShapeDtypeStruct((NX * NY, slab + 8, half), jnp.bfloat16),
        compiler_params=pltpu.CompilerParams(vmem_limit_bytes=16 * MIB),
        name="pack",
    )(own, got, mass, mass_got)


def repack_kernel(slab, got_ref, out_ref):
    n_slabs, rows = got_ref.shape[0], slab // NZ
    total = got_ref[0].astype(jnp.float32)
    for k in range(1, n_slabs):
        total += got_ref[k].astype(jnp.float32)
    out_ref[:, :rows, :] = total[:slab].reshape(NZ, rows, total.shape[1])
    extra = total[slab:]
    extra = extra + pltpu.roll(extra, 6, 0) + pltpu.roll(extra, 4, 0)
    for k in range(NZ):
        out_ref[k, rows:, :] = extra


def repack_call(got, slab):
    half = got.shape[2]
    return pl.pallas_call(
        functools.partial(repack_kernel, slab),
        in_specs=[pl.BlockSpec(memory_space=pltpu.VMEM)],
        out_specs=pl.BlockSpec(memory_space=pltpu.VMEM),
        out_shape=jax.ShapeDtypeStruct((NZ, slab // NZ + 8, half), jnp.float32),
        compiler_params=pltpu.CompilerParams(vmem_limit_bytes=16 * MIB),
        name="repack",
    )(got)


def finish_kernel(rows, place_ref, got_ref, out_ref, mass_ref):
    total = got_ref[0]
    for k in range(1, got_ref.shape[0]):
        total += got_ref[k]
    half = total.shape[1]
    place = place_ref[0]
    mass = total[rows:]
    mass_ref[...] = mass
    part = place // half
    row = jnp.where(part == 0, mass[0:1], mass[1:2])
    lane = lax.broadcasted_iota(jnp.int32, (rows, half), 1)
    first = place - part * half
    mine = lane == first + lax.broadcasted_iota(jnp.int32, (rows, half), 0)
    own_mass = jnp.sum(jnp.where(mine, jnp.broadcast_to(row, (rows, half)), 0.0), axis=1, keepdims=True)
    centroids = (total[:rows] / own_mass).astype(jnp.bfloat16)
    for k in range(out_ref.shape[0]):
        out_ref[k] = centroids


def finish_call(got, place, rows):
    half = got.shape[2]
    return pl.pallas_call(
        functools.partial(finish_kernel, rows),
        grid_spec=pltpu.PrefetchScalarGridSpec(
            num_scalar_prefetch=1,
            grid=(1,),
            in_specs=[pl.BlockSpec(got.shape, lambda i, place: (0, 0, 0))],
            out_specs=[
                pl.BlockSpec((NX * NZ, rows, half), lambda i, place: (0, 0, 0)),
                pl.BlockSpec((8, half), lambda i, place: (0, 0)),
            ],
        ),
        out_shape=[
            jax.ShapeDtypeStruct((NX * NZ, rows, half), jnp.bfloat16),
            jax.ShapeDtypeStruct((8, half), jnp.float32),
        ],
        compiler_params=pltpu.CompilerParams(vmem_limit_bytes=16 * MIB),
        name="finish",
    )(place, got)


def join_kernel(core_ref, block_ref, other_ref, out_ref):
    half = block_ref.shape[1]
    core = core_ref[0]
    out_ref[:, pl.ds(pl.multiple_of(core * half, half), half)] = block_ref[...]
    out_ref[:, pl.ds(pl.multiple_of((1 - core) * half, half), half)] = other_ref[...]


def join_call(core, block, other):
    rows, half = block.shape
    return pl.pallas_call(
        join_kernel,
        grid_spec=pltpu.PrefetchScalarGridSpec(
            num_scalar_prefetch=1,
            grid=(1,),
            in_specs=[pl.BlockSpec((rows, half), lambda i, core: (0, 0))] * 2,
            out_specs=pl.BlockSpec((rows, 2 * half), lambda i, core: (0, 0)),
        ),
        out_shape=jax.ShapeDtypeStruct((rows, 2 * half), jnp.bfloat16),
        compiler_params=pltpu.CompilerParams(vmem_limit_bytes=16 * MIB),
        name="join",
    )(core, block, other)


def per_device(documents, centroids, cluster_mass):
    n_docs = documents.shape[0] * NX * NZ * NC * NY
    n_clusters = centroids.shape[0]
    half = documents.shape[1] // NC
    core = lax.axis_index("c")
    slab = n_clusters // (NX * NY)
    rows = slab // NZ
    place = (lax.axis_index("y") * NX + lax.axis_index("x")) * slab + lax.axis_index("z") * rows
    loga = -math.log(n_docs)
    documents, core, place = lax.optimization_barrier((documents, core.reshape(1), place.reshape(1)))

    def duals_of(column_mass):
        return TAU * (jnp.log(cluster_mass) - jnp.log(column_mass.reshape(n_clusters)))

    def everywhere(mass):
        return sum_all(mass.reshape(n_clusters // LANES, LANES))

    scores, mass = first_call(documents, centroids, loga)
    duals = duals_of(everywhere(mass)).reshape(1, n_clusters)
    mass = middle_call(scores, duals, loga)
    duals = duals_of(everywhere(mass)).reshape(1, n_clusters)
    send, own, mass = last_call(scores, duals, documents, core, loga)
    packed = pack_call(own, swap_cores(send), mass, swap_cores(mass))
    packed = repack_call(lax.all_to_all(packed, ("y", "x"), 0, 0, tiled=True), slab)
    packed = lax.all_to_all(packed, ("z",), 0, 0, tiled=True)
    mine, column_mass = finish_call(packed, place, rows)
    block = lax.all_to_all(mine, ("x", "z"), 0, 0, tiled=True).reshape(n_clusters // NY, half)
    return join_call(core, block, swap_cores(block)), duals_of(column_mass[:2])


def solution(mesh):
    grid = Mesh(mesh.devices.reshape(NX, NZ, NC, NY), AXES)
    return jax.shard_map(
        per_device,
        mesh=grid,
        in_specs=(P(AXES, None), P(), P()),
        out_specs=(P("y", None), P()),
        check_vma=False,
    )
```

time: 443 us -> 151 us (0.34)
  waiting for transfers between devices: 152 us -> 2.7 us
  blocking collectives: 230 us -> 100 us
  Pallas kernels: 0 us -> 38.6 us
  other arithmetic: 26 us -> 1.89 us
  between operations: 14.2 us -> 0.69 us
  matrix products: 12.5 us -> 0 us
    psum x3 -> x0, blocking collectives: 230 us -> none  [per_device(): column_mass = lax.psum(jnp.sum(mass, axis=0), ('rows', 'sub'))]
    psum x1 -> x0, waiting for transfers between devices: 107 us -> none  [per_device(): lax.psum(lax.dot_general(plan, documents, (((0,), (0,)), ((), ())), prefe...]
    all_to_all x0 -> x7, blocking collectives: none -> 100 us  [the longest x4 53.2 us: broadcast_to_group(): lax.all_to_all(jnp.broadcast_to(value[None], (size, *value.shape)), axes,...]
    reduce_scatter x1 -> x0, waiting for transfers between devices: 45.1 us -> none  [per_device(): own = lax.psum_scatter(total, 'sub', scatter_dimension=0, tiled=True)]
    pallas_call x0 -> x7, Pallas kernels: none -> 38.6 us  [the longest x1 15.1 us: last_call(): pl.pallas_call(functools.partial(last_kernel, loga, n_blocks, n_tiles), g...]
    reduce_sum x6 -> x4, other arithmetic: 14.9 us -> 0.07 us  [the longest x2 0.04 us: sum_all(): value = jnp.sum(broadcast_to_group(value, ('x', 'y'), NX * NY), axis=0)]
    dot_general x2 -> x0, matrix products: 12.5 us -> none  [the longest x1 6.38 us: per_device(): lax.dot_general(documents, centroids, (((1,), (1,)), ((), ())), preferred...]
    reduce_max x2 -> x0, other arithmetic: 8.3 us -> none  [per_device(): lse = jax.nn.logsumexp(scores + duals[None, :], axis=1)]
  transfers between devices with their start and end apart: 2 -> 3, of which waited for: 2 -> 2; matrix products, arithmetic and copies ran while one was open for 1% -> 0% of each run, Pallas kernels for 0% -> 0%
where the time goes in v2:
time: 151 us; the launch traced here: 150 us
  blocking collectives  100 us (66%)
  Pallas kernels  38.6 us (26%)
  starting transfers between devices  4.35 us (3%)
  waiting for transfers between devices  2.7 us (2%)
  other arithmetic  1.89 us (1%)
    all_to_all x4, blocking collectives, broadcast_to_group(): lax.all_to_all(jnp.broadcast_to(value[None], (size, *value.shape)), axes,...  53.2 us
    all_to_all x1, blocking collectives, per_device(): lax.all_to_all(packed, ('y', 'x'), 0, 0, tiled=True)  21.2 us
    pallas_call x1, Pallas kernels, last_call(): pl.pallas_call(functools.partial(last_kernel, loga, n_blocks, n_tiles), g...  15.1 us
    pallas_call x1, Pallas kernels, first_call(): pl.pallas_call(functools.partial(first_kernel, loga, n_blocks), grid=(n_b...  13.7 us
    all_to_all x1, blocking collectives, per_device(): lax.all_to_all(mine, ('x', 'z'), 0, 0, tiled=True)  13.1 us
    all_to_all x1, blocking collectives, per_device(): packed = lax.all_to_all(packed, ('z',), 0, 0, tiled=True)  12.6 us
    pallas_call x1, Pallas kernels, middle_call(): pl.pallas_call(functools.partial(middle_kernel, loga, n_blocks), grid=(n_...  8.42 us
    ppermute x3, starting transfers between devices, swap_cores(): return lax.ppermute(value, 'c', [(0, 1), (1, 0)])  4.35 us
  transfers between devices with their start and end apart: 3, of which 2 were waited for; matrix products, arithmetic and copies ran while one was open for 0% of the time, Pallas kernels for 0%

profile of v2, /device:TPU:1, one launch (start us, length us, event | category | flops | bytes accessed | tf_op | source)
XLA Modules:
  0.0 149.8 jit_solution(111844810579104700)
XLA Ops:
  0.6 0.0 copy-start
  0.6 13.7 %first.1 = (f32[1024,2048]{1,0:T(8,128)}, f32[1,1024]{1,0:T(1,128)}) custom-call(bf16[2048,1024]{1,0:T(8,128)(2,1)} %docs_ref.1, bf16[1024,1024]{1,0:T(8,128)(2,1)} %cent_ref.1), custom_call_target="tpu_custom_call" | custom-call | tf_op jit(solution)/shard_map/first/pallas_call | solution.py:72
  14.4 0.7 broadcast_in_dim.13
  15.1 13.9 %all_to_all.35 = f32[16,8,128]{2,1,0:T(8,128)S(1)} all-to-all(f32[16,8,128]{2,1,0:T(8,128)S(1)} %broadcast_in_dim.13), channel_id=1, replica_groups=mesh['x'=4,'z'=8,'c'=2,'y'=4] {'x','y'}, dimensions={0} | all-to-all | bytes 131072 | tf_op jit(solution)/shard_map/all_to_all | solution.py:28
  29.0 18.2 %all_to_all.36 = f32[16,8,128]{2,1,0:T(8,128)S(1)} all-to-all(f32[16,8,128]{2,1,0:T(8,128)S(1)} %broadcast_in_dim.28), channel_id=1, replica_groups=mesh['x'=4,'z'=8,'c'=2,'y'=4] {'z','c'}, dimensions={0} | all-to-all | bytes 131072 | tf_op jit(solution)/shard_map/all_to_all | solution.py:28
  47.1 0.0 copy-done
  47.2 0.6 fusion.1
  47.8 8.4 %middle.1 = f32[1,1024]{1,0:T(1,128)} custom-call(f32[1024,2048]{1,0:T(8,128)} %get-tuple-element.15.scores_ref, f32[1,1024]{1,0:T(1,128)} %bitcast.20), custom_call_target="tpu_custom_call" | custom-call | tf_op jit(solution)/shard_map/middle/pallas_call | solution.py:122
  56.2 0.7 broadcast_in_dim.30
  56.9 9.4 %all_to_all.37 = f32[16,8,128]{2,1,0:T(8,128)S(1)} all-to-all(f32[16,8,128]{2,1,0:T(8,128)S(1)} %broadcast_in_dim.30), channel_id=1, replica_groups=mesh['x'=4,'z'=8,'c'=2,'y'=4] {'x','y'}, dimensions={0} | all-to-all | bytes 131072 | tf_op jit(solution)/shard_map/all_to_all | solution.py:28
  66.3 11.8 %all_to_all.38 = f32[16,8,128]{2,1,0:T(8,128)S(1)} all-to-all(f32[16,8,128]{2,1,0:T(8,128)S(1)} %broadcast_in_dim.31), channel_id=1, replica_groups=mesh['x'=4,'z'=8,'c'=2,'y'=4] {'z','c'}, dimensions={0} | all-to-all | bytes 131072 | tf_op jit(solution)/shard_map/all_to_all | solution.py:28
  78.1 0.6 fusion
  78.7 15.1 %last.1 = (bf16[1024,512]{1,0:T(8,128)(2,1)S(1)}, f32[1024,512]{1,0:T(8,128)S(1)}, f32[1,1024]{1,0:T(1,128)S(1)}) custom-call(s32[1]{0:T(128)} %bitcast.core_ref, f32[1024,2048]{1,0:T(8,128)} %get-tuple-element.15.scores_ref, f32[1,1024]{1,0:T(1,128)} %bitcast.22, bf16[2048,1024]{1,0:T(8,128)(2,1)} %docs_ref.1), custom_call_target="tpu_custom_call" | custom-call | tf_op jit(solution)/shard_map/last/pallas_call | solution.py:186
  93.8 0.2 collective-permute-start
  94.1 0.3 collective-permute-start.1
  94.4 2.2 %collective-permute-done.1.mass_got_ref = f32[1,1024]{1,0:T(1,128)S(1)} collective-permute-done((f32[1,1024]{1,0:T(1,128)S(1)}, f32[1,1024]{1,0:T(1,128)S(1)}, u32[]{:S(2)}, u32[]{:S(2)}) %collective-permute-start.1) | collective-permute-done | bytes 4128 | tf_op jit(solution)/shard_map/ppermute | solution.py:24
  96.6 0.0 collective-permute-done.got_ref
  96.6 0.3 pack.1
  96.9 21.2 %all_to_all.39.got_ref = bf16[16,72,512]{2,1,0:T(8,128)(2,1)S(1)} all-to-all(bf16[16,72,512]{2,1,0:T(8,128)(2,1)S(1)} %pack.1), channel_id=1, replica_groups=mesh['x'=4,'z'=8,'c'=2,'y'=4] {'y','x'}, dimensions={0} | all-to-all | bytes 2359296 | tf_op jit(solution)/shard_map/all_to_all | solution.py:368
  118.0 0.2 repack.1
  118.2 12.6 %all_to_all.40.got_ref = f32[8,16,512]{2,1,0:T(8,128)S(1)} all-to-all(f32[8,16,512]{2,1,0:T(8,128)S(1)} %repack.1), channel_id=1, replica_groups=mesh['x'=4,'z'=8,'c'=2,'y'=4] {'z'}, dimensions={0} | all-to-all | bytes 524288 | tf_op jit(solution)/shard_map/all_to_all | solution.py:369
  130.8 0.1 finish.1
  130.9 13.1 %all_to_all.41 = bf16[32,8,512]{2,1,0:T(8,128)(2,1)S(1)} all-to-all(bf16[32,8,512]{2,1,0:T(8,128)(2,1)S(1)} %get-tuple-element.20), channel_id=1, replica_groups=mesh['x'=4,'z'=8,'c'=2,'y'=4] {'x','z'}, dimensions={0} | all-to-all | bytes 524288 | tf_op jit(solution)/shard_map/all_to_all | solution.py:371
  144.1 3.8 %collective-permute-start.2 = (bf16[256,512]{1,0:T(8,128)(2,1)S(1)}, bf16[256,512]{1,0:T(8,128)(2,1)S(1)}, u32[]{:S(2)}, u32[]{:S(2)}) collective-permute-start(bf16[256,512]{1,0:T(8,128)(2,1)S(1)} %bitcast.18), channel_id=1, source_target_pairs={{0,4},{4,0},{1,5},{5,1},{2,6},{6,2},{3,7},{7,3},{8,12},{12,8},{9,1... | collective-permute-start | bytes 786440 | tf_op jit(solution)/shard_map/ppermute | solution.py:24
  147.8 0.6 subtract_multiply_fusion
  148.4 0.5 collective-permute-done.2.other_ref
  149.0 0.8 join.1
  (8 shorter events, 0.1 us)
Async XLA Ops:
  0.6 46.5 %copy-start = (f32[1024]{0:T(1024)S(1)}, f32[1024]{0:T(1024)}, u32[]{:S(2)}) copy-start(f32[1024]{0:T(1024)} %param.5) | copy-start | bytes 12292
  93.8 2.8 %collective-permute-start = (bf16[1024,512]{1,0:T(8,128)(2,1)S(1)}, bf16[1024,512]{1,0:T(8,128)(2,1)S(1)}, u32[]{:S(2)}, u32[]{:S(2)}) collective-permute-start(bf16[1024,512]{1,0:T(8,128)(2,1)S(1)} %get-tuple-element.18), channel_id=1, source_target_pairs={{0,4},{4,0},{1,5},{5,1},{2,6},{6,2},{3,7},{7,3},{8,12},{12,8},{9,1... | collective-permute-start | bytes 3145736 | tf_op jit(solution)/shard_map/ppermute | solution.py:24
  94.1 2.5 %collective-permute-start.1 = (f32[1,1024]{1,0:T(1,128)S(1)}, f32[1,1024]{1,0:T(1,128)S(1)}, u32[]{:S(2)}, u32[]{:S(2)}) collective-permute-start(f32[1,1024]{1,0:T(1,128)S(1)} %get-tuple-element.19.mass_ref), channel_id=1, source_target_pairs={{0,4},{4,0},{1,5},{5,1},{2,6},{6,2},{3,7},{7,3},{8,12},{12,8},{9,1... | collective-permute-start | bytes 12296 | tf_op jit(solution)/shard_map/ppermute | solution.py:24
  144.1 4.9 %collective-permute-start.2 = (bf16[256,512]{1,0:T(8,128)(2,1)S(1)}, bf16[256,512]{1,0:T(8,128)(2,1)S(1)}, u32[]{:S(2)}, u32[]{:S(2)}) collective-permute-start(bf16[256,512]{1,0:T(8,128)(2,1)S(1)} %bitcast.18), channel_id=1, source_target_pairs={{0,4},{4,0},{1,5},{5,1},{2,6},{6,2},{3,7},{7,3},{8,12},{12,8},{9,1... | collective-permute-start | bytes 786440 | tf_op jit(solution)/shard_map/ppermute | solution.py:24

commit v3 on v0

v3 whole, which is shorter than its diff:
```python
import functools
import math

import jax
import jax.numpy as jnp
from jax import lax
from jax.experimental import pallas as pl
from jax.experimental.pallas import tpu as pltpu
from jax.sharding import Mesh
from jax.sharding import PartitionSpec as P

D = 1024
TAU = 0.8
TEMP = 4.0
NX, NZ, NC, NY = 4, 8, 2, 4
AXES = ("x", "z", "c", "y")
LANES = 128
BLOCK = 512
CHUNK = 64
LOG2E = 1 / math.log(2)
TILE = 256
MIB = 2**20


def swap_cores(value):
    return lax.ppermute(value, "c", [(0, 1), (1, 0)])


def fold(value, op):
    return op(value.reshape(value.shape[0] // 8, 8, value.shape[1]), axis=0)


def block_masses(scores_ref, columns, duals_ref, loga, emit):
    n_clusters = scores_ref.shape[0]
    width = columns.stop - columns.start

    def shifted(row):
        value = scores_ref[row : row + CHUNK, columns]
        if duals_ref is None:
            return value
        duals = duals_ref[row : row + CHUNK, :]
        return value + jnp.concatenate([duals] * (width // LANES), axis=1)

    top = fold(shifted(0), jnp.max)
    for row in range(CHUNK, n_clusters, CHUNK):
        top = jnp.maximum(top, fold(shifted(row), jnp.max))
    top = jnp.max(top, axis=0, keepdims=True)
    total = fold(jnp.exp2(shifted(0) - top), jnp.sum)
    for row in range(CHUNK, n_clusters, CHUNK):
        total += fold(jnp.exp2(shifted(row) - top), jnp.sum)
    lse = top + jnp.log2(jnp.sum(total, axis=0, keepdims=True))
    row_duals = TAU * (loga - lse)
    for row in range(0, n_clusters, CHUNK):
        emit(row, jnp.exp2(scores_ref[row : row + CHUNK, columns] + row_duals))


def add_lanes(acc, row, mass):
    total = mass[:, :LANES]
    for lane in range(LANES, mass.shape[1], LANES):
        total += mass[:, lane : lane + LANES]
    acc[row : row + CHUNK, :] += total


def column_sums(acc, out_ref):
    rows = [jnp.sum(acc[k : k + LANES, :].T, axis=0, keepdims=True) for k in range(0, acc.shape[0], LANES)]
    sums = jnp.concatenate(rows, axis=0)
    for slot in range(out_ref.shape[0]):
        out_ref[slot] = sums


def start_duals(got_ref, cluster_mass_ref, duals_col):
    column_mass = got_ref[0]
    for slot in range(1, got_ref.shape[0]):
        column_mass += got_ref[slot]
    duals = TAU * (jnp.log2(cluster_mass_ref[...]) - jnp.log2(column_mass))
    for k in range(duals.shape[0]):
        row = jnp.broadcast_to(duals[k : k + 1, :], (LANES, LANES))
        duals_col[k * LANES : (k + 1) * LANES, :] = row.T


def first_kernel(loga, docs_hbm, cent_hbm, scores_ref, mass_ref, docs_ref, cent_ref, acc, sems):
    n_blocks = scores_ref.shape[0]
    copies = [pltpu.make_async_copy(cent_hbm, cent_ref, sems.at[n_blocks])]
    for block in range(n_blocks):
        rows = pl.ds(block * BLOCK, BLOCK)
        copies.append(pltpu.make_async_copy(docs_hbm.at[rows], docs_ref.at[rows], sems.at[block]))
    for copy in copies:
        copy.start()
    acc[...] = jnp.zeros_like(acc)
    copies[0].wait()
    for block in range(n_blocks + 1):
        if block < n_blocks:
            copies[block + 1].wait()
            scores_ref[block] = lax.dot_general(
                cent_ref[...],
                docs_ref[block * BLOCK : (block + 1) * BLOCK, :],
                (((1,), (1,)), ((), ())),
                preferred_element_type=jnp.float32,
            ) * (TEMP / math.sqrt(D) * LOG2E)
        if block > 0:
            block_masses(scores_ref.at[block - 1], slice(0, BLOCK), None, loga, functools.partial(add_lanes, acc))
    column_sums(acc, mass_ref)


def first_call(documents, centroids, loga):
    n_docs, dim = documents.shape
    n_clusters = centroids.shape[0]
    n_blocks = n_docs // BLOCK
    vmem = pl.BlockSpec(memory_space=pltpu.VMEM)
    return pl.pallas_call(
        functools.partial(first_kernel, loga),
        in_specs=[pl.BlockSpec(memory_space=pltpu.HBM)] * 2,
        out_specs=[vmem] * 3,
        out_shape=[
            pltpu.VMEM((n_blocks, n_clusters, BLOCK), jnp.float32),
            pltpu.VMEM((NX * NY, n_clusters // LANES, LANES), jnp.float32),
            pltpu.VMEM((n_docs, dim), jnp.bfloat16),
        ],
        scratch_shapes=[
            pltpu.VMEM((n_clusters, dim), jnp.bfloat16),
            pltpu.VMEM((n_clusters, LANES), jnp.float32),
            pltpu.SemaphoreType.DMA((n_blocks + 1,)),
        ],
        compiler_params=pltpu.CompilerParams(vmem_limit_bytes=50 * MIB),
        name="first",
    )(documents, centroids)


def middle_kernel(loga, scores_ref, got_ref, cluster_mass_ref, mass_ref, duals_col, acc):
    start_duals(got_ref, cluster_mass_ref, duals_col)
    acc[...] = jnp.zeros_like(acc)

    @pl.loop(0, scores_ref.shape[0])
    def _(block):
        block_masses(scores_ref.at[block], slice(0, BLOCK), duals_col, loga, functools.partial(add_lanes, acc))

    column_sums(acc, mass_ref)


def middle_call(scores, got, cluster_mass, loga):
    n_clusters = scores.shape[1]
    vmem = pl.BlockSpec(memory_space=pltpu.VMEM)
    return pl.pallas_call(
        functools.partial(middle_kernel, loga),
        in_specs=[vmem] * 3,
        out_specs=vmem,
        out_shape=pltpu.VMEM((NX * NY, n_clusters // LANES, LANES), jnp.float32),
        scratch_shapes=[
            pltpu.VMEM((n_clusters, LANES), jnp.float32),
            pltpu.VMEM((n_clusters, LANES), jnp.float32),
        ],
        compiler_params=pltpu.CompilerParams(vmem_limit_bytes=8 * MIB),
        name="middle",
    )(scores, got, cluster_mass)


def last_kernel(loga, core_ref, scores_ref, got_ref, cluster_mass_ref, docs_ref, send_ref, own_ref, mass_ref, plan, duals_col, acc):
    start_duals(got_ref, cluster_mass_ref, duals_col)
    acc[...] = jnp.zeros_like(acc)

    @pl.loop(0, scores_ref.shape[0])
    def _(block):
        def emit(row, mass):
            add_lanes(acc, row, mass)
            columns = pl.ds(pl.multiple_of(block * BLOCK, BLOCK), BLOCK)
            plan[row : row + CHUNK, columns] = mass.astype(jnp.bfloat16)

        block_masses(scores_ref.at[block], slice(0, BLOCK), duals_col, loga, emit)

    column_sums(acc, mass_ref)
    half = own_ref.shape[1]
    for out_ref, owner in ((send_ref, 1 - core_ref[0]), (own_ref, core_ref[0])):
        for tile in range(0, half, TILE):
            columns = pl.ds(pl.multiple_of(owner * half + tile, TILE), TILE)
            out_ref[:, tile : tile + TILE] = lax.dot_general(
                plan[...], docs_ref[:, columns], (((1,), (0,)), ((), ())), preferred_element_type=jnp.float32
            ).astype(out_ref.dtype)


def last_call(scores, got, cluster_mass, documents, core, loga):
    n_clusters = scores.shape[1]
    n_docs, dim = documents.shape
    half = dim // NC
    vmem = pl.BlockSpec(memory_space=pltpu.VMEM)
    return pl.pallas_call(
        functools.partial(last_kernel, loga),
        in_specs=[pl.BlockSpec(memory_space=pltpu.SMEM)] + [vmem] * 4,
        out_specs=[vmem] * 3,
        out_shape=[
            pltpu.VMEM((n_clusters, half), jnp.bfloat16),
            pltpu.VMEM((n_clusters, half), jnp.float32),
            pltpu.VMEM((1, n_clusters // LANES, LANES), jnp.float32),
        ],
        scratch_shapes=[
            pltpu.VMEM((n_clusters, n_docs), jnp.bfloat16),
            pltpu.VMEM((n_clusters, LANES), jnp.float32),
            pltpu.VMEM((n_clusters, LANES), jnp.float32),
        ],
        compiler_params=pltpu.CompilerParams(vmem_limit_bytes=20 * MIB),
        name="last",
    )(core, scores, got, cluster_mass, documents)


def sum_kernel(got_ref, out_ref):
    total = got_ref[0]
    for slot in range(1, got_ref.shape[0]):
        total += got_ref[slot]
    for slot in range(out_ref.shape[0]):
        out_ref[slot] = total


def sum_call(got, copies):
    vmem = pl.BlockSpec(memory_space=pltpu.VMEM)
    return pl.pallas_call(
        sum_kernel,
        in_specs=[vmem],
        out_specs=vmem,
        out_shape=pltpu.VMEM((copies, *got.shape[1:]), got.dtype),
        compiler_params=pltpu.CompilerParams(vmem_limit_bytes=4 * MIB),
        name="sum",
    )(got)


def pack_kernel(own_ref, got_ref, mass_ref, mass_got_ref, out_ref):
    half = own_ref.shape[1]
    n_slabs = out_ref.shape[0]
    slab = own_ref.shape[0] // n_slabs
    mass = mass_ref[0] + mass_got_ref[0]
    high = mass.astype(jnp.bfloat16)
    middle = (mass - high.astype(jnp.float32)).astype(jnp.bfloat16)
    low = (mass - high.astype(jnp.float32) - middle.astype(jnp.float32)).astype(jnp.bfloat16)
    rest = jnp.zeros((mass.shape[0], half - 3 * LANES), jnp.bfloat16)
    extra = jnp.concatenate([high, middle, low, rest], axis=1)
    for k in range(n_slabs):
        rows = slice(k * slab, (k + 1) * slab)
        out_ref[k, :slab, :] = (own_ref[rows, :] + got_ref[rows, :].astype(jnp.float32)).astype(jnp.bfloat16)
        out_ref[k, slab:, :] = extra


def pack_call(own, got, mass, mass_got):
    n_clusters, half = own.shape
    n_slabs = NX * NY
    vmem = pl.BlockSpec(memory_space=pltpu.VMEM)
    return pl.pallas_call(
        pack_kernel,
        in_specs=[vmem] * 4,
        out_specs=vmem,
        out_shape=pltpu.VMEM((n_slabs, n_clusters // n_slabs + mass.shape[1], half), jnp.bfloat16),
        compiler_params=pltpu.CompilerParams(vmem_limit_bytes=8 * MIB),
        name="pack",
    )(own, got, mass, mass_got)


def repack_kernel(slab, got_ref, out_ref):
    rows = slab // NZ
    total = got_ref[0].astype(jnp.float32)
    for k in range(1, got_ref.shape[0]):
        total += got_ref[k].astype(jnp.float32)
    extra = total[slab:]
    extra = extra + jnp.concatenate([extra[:, LANES:], extra[:, :LANES]], axis=1) + jnp.concatenate(
        [extra[:, 2 * LANES :], extra[:, : 2 * LANES]], axis=1
    )
    for k in range(NZ):
        out_ref[k, :rows, :] = total[k * rows : (k + 1) * rows]
        out_ref[k, rows:, :] = extra


def repack_call(got, slab):
    vmem = pl.BlockSpec(memory_space=pltpu.VMEM)
    shape = (NZ, slab // NZ + got.shape[1] - slab, got.shape[2])
    return pl.pallas_call(
        functools.partial(repack_kernel, slab),
        in_specs=[vmem],
        out_specs=vmem,
        out_shape=pltpu.VMEM(shape, jnp.float32),
        compiler_params=pltpu.CompilerParams(vmem_limit_bytes=8 * MIB),
        name="repack",
    )(got)


def finish_kernel(rows, place_ref, got_ref, cluster_mass_ref, out_ref, duals_ref):
    total = got_ref[0]
    for k in range(1, got_ref.shape[0]):
        total += got_ref[k]
    mass = total[rows:, :LANES]
    duals_ref[...] = TAU * (jnp.log(cluster_mass_ref[...]) - jnp.log(mass))
    place = place_ref[0]
    group = place // LANES
    first = place - group * LANES
    row = lax.broadcasted_iota(jnp.int32, mass.shape, 0)
    lane = lax.broadcasted_iota(jnp.int32, mass.shape, 1)
    line = jnp.sum(jnp.where(row == group, mass, 0.0), axis=0, keepdims=True)
    mine = jnp.where(lane == row + first, jnp.broadcast_to(line, mass.shape), 0.0)
    own_mass = jnp.sum(mine, axis=1, keepdims=True)
    centroids = (total[:rows] / own_mass).astype(jnp.bfloat16)
    for k in range(out_ref.shape[0]):
        out_ref[k] = centroids


def finish_call(got, cluster_mass, place, rows):
    half = got.shape[2]
    vmem = pl.BlockSpec(memory_space=pltpu.VMEM)
    return pl.pallas_call(
        functools.partial(finish_kernel, rows),
        in_specs=[pl.BlockSpec(memory_space=pltpu.SMEM), vmem, vmem],
        out_specs=[vmem, vmem],
        out_shape=[
            pltpu.VMEM((NX * NZ, rows, half), jnp.bfloat16),
            jax.ShapeDtypeStruct(cluster_mass.shape, jnp.float32),
        ],
        compiler_params=pltpu.CompilerParams(vmem_limit_bytes=8 * MIB),
        name="finish",
    )(place, got, cluster_mass)


def join_kernel(core_ref, block_ref, other_ref, out_ref):
    half = block_ref.shape[1]
    core = core_ref[0]
    out_ref[:, pl.ds(pl.multiple_of(core * half, half), half)] = block_ref[...]
    out_ref[:, pl.ds(pl.multiple_of((1 - core) * half, half), half)] = other_ref[...]


def join_call(core, block, other):
    rows, half = block.shape
    vmem = pl.BlockSpec(memory_space=pltpu.VMEM)
    return pl.pallas_call(
        join_kernel,
        in_specs=[pl.BlockSpec(memory_space=pltpu.SMEM), vmem, vmem],
        out_specs=vmem,
        out_shape=jax.ShapeDtypeStruct((rows, 2 * half), jnp.bfloat16),
        compiler_params=pltpu.CompilerParams(vmem_limit_bytes=8 * MIB),
        name="join",
    )(core, block, other)


def sum_all(copies):
    got = lax.all_to_all(copies, ("x", "y"), 0, 0, tiled=True)
    return lax.all_to_all(sum_call(got, NZ * NC), ("z", "c"), 0, 0, tiled=True)


def per_device(documents, centroids, cluster_mass):
    n_docs = documents.shape[0] * NX * NZ * NC * NY
    n_clusters = centroids.shape[0]
    half = documents.shape[1] // NC
    core = lax.axis_index("c")
    slab = n_clusters // (NX * NY)
    rows = slab // NZ
    place = (lax.axis_index("y") * NX + lax.axis_index("x")) * slab + lax.axis_index("z") * rows
    documents, core, place = lax.optimization_barrier((documents, core.reshape(1), place.reshape(1)))
    loga = -math.log2(n_docs)
    cluster_mass = cluster_mass.reshape(n_clusters // LANES, LANES)
    scores, mass, documents = first_call(documents, centroids, loga)
    mass = middle_call(scores, sum_all(mass), cluster_mass, loga)
    send, own, mass = last_call(scores, sum_all(mass), cluster_mass, documents, core, loga)
    packed = pack_call(own, swap_cores(send), mass, swap_cores(mass))
    packed = repack_call(lax.all_to_all(packed, ("y", "x"), 0, 0, tiled=True), slab)
    packed = lax.all_to_all(packed, ("z",), 0, 0, tiled=True)
    mine, duals = finish_call(packed, cluster_mass, place, rows)
    block = lax.all_to_all(mine, ("x", "z"), 0, 0, tiled=True).reshape(n_clusters // NY, half)
    return join_call(core, block, swap_cores(block)), duals.reshape(n_clusters)


def solution(mesh):
    grid = Mesh(mesh.devices.reshape(NX, NZ, NC, NY), AXES)
    return jax.shard_map(
        per_device,
        mesh=grid,
        in_specs=(P(AXES, None), P(), P()),
        out_specs=(P("y", None), P()),
        check_vma=False,
    )
```

time: 443 us -> 131 us (0.30)
  waiting for transfers between devices: 152 us -> 3.32 us
  blocking collectives: 230 us -> 100 us
  other arithmetic: 26 us -> 0 us
  Pallas kernels: 0 us -> 21.9 us
  between operations: 14.2 us -> 0.68 us
  matrix products: 12.5 us -> 0 us
  local copies, waits for them, and re-layouts: 5.75 us -> 0.01 us
    psum x3 -> x0, blocking collectives: 230 us -> none  [per_device(): column_mass = lax.psum(jnp.sum(mass, axis=0), ('rows', 'sub'))]
    psum x1 -> x0, waiting for transfers between devices: 107 us -> none  [per_device(): lax.psum(lax.dot_general(plan, documents, (((0,), (0,)), ((), ())), prefe...]
    all_to_all x0 -> x7, blocking collectives: none -> 100 us  [the longest x2 29.9 us: sum_all(): return lax.all_to_all(sum_call(got, NZ * NC), ('z', 'c'), 0, 0, tiled=True)]
    reduce_scatter x1 -> x0, waiting for transfers between devices: 45.1 us -> none  [per_device(): own = lax.psum_scatter(total, 'sub', scatter_dimension=0, tiled=True)]
    pallas_call x0 -> x9, Pallas kernels: none -> 21.9 us  [the longest x1 8.76 us: first_call(): pl.pallas_call(functools.partial(first_kernel, loga), in_specs=[pl.BlockS...]
    reduce_sum x6 -> x0, other arithmetic: 14.9 us -> none  [the longest x3 7.93 us: per_device(): lse = jax.nn.logsumexp(scores + duals[None, :], axis=1)]
    dot_general x2 -> x0, matrix products: 12.5 us -> none  [the longest x1 6.38 us: per_device(): lax.dot_general(documents, centroids, (((1,), (1,)), ((), ())), preferred...]
    reduce_max x2 -> x0, other arithmetic: 8.3 us -> none  [per_device(): lse = jax.nn.logsumexp(scores + duals[None, :], axis=1)]
  transfers between devices with their start and end apart: 2 -> 3, of which waited for: 2 -> 2; matrix products, arithmetic and copies ran while one was open for 1% -> 0% of each run, Pallas kernels for 0% -> 0%
where the time goes in v3:
time: 131 us; the launch traced here: 130 us
  blocking collectives  100 us (76%)
  Pallas kernels  21.9 us (17%)
  starting transfers between devices  4.35 us (3%)
  waiting for transfers between devices  3.32 us (3%)
    all_to_all x2, blocking collectives, sum_all(): return lax.all_to_all(sum_call(got, NZ * NC), ('z', 'c'), 0, 0, tiled=True)  29.9 us
    all_to_all x2, blocking collectives, sum_all(): got = lax.all_to_all(copies, ('x', 'y'), 0, 0, tiled=True)  23.4 us
    all_to_all x1, blocking collectives, per_device(): lax.all_to_all(packed, ('y', 'x'), 0, 0, tiled=True)  21.2 us
    all_to_all x1, blocking collectives, per_device(): lax.all_to_all(mine, ('x', 'z'), 0, 0, tiled=True)  13.1 us
    all_to_all x1, blocking collectives, per_device(): packed = lax.all_to_all(packed, ('z',), 0, 0, tiled=True)  12.6 us
    pallas_call x1, Pallas kernels, first_call(): pl.pallas_call(functools.partial(first_kernel, loga), in_specs=[pl.BlockS...  8.76 us
    pallas_call x1, Pallas kernels, last_call(): pl.pallas_call(functools.partial(last_kernel, loga), in_specs=[pl.BlockSp...  7.76 us
    ppermute x3, starting transfers between devices, swap_cores(): return lax.ppermute(value, 'c', [(0, 1), (1, 0)])  4.35 us
  transfers between devices with their start and end apart: 3, of which 2 were waited for; matrix products, arithmetic and copies ran while one was open for 0% of the time, Pallas kernels for 0%

profile of v3, /device:TPU:1, one launch (start us, length us, event | category | flops | bytes accessed | tf_op | source)
XLA Modules:
  0.0 130.4 jit_solution(11385311311167065307)
XLA Ops:
  0.6 0.0 copy-start
  0.6 8.8 %first.1 = (f32[4,1024,512]{2,1,0:T(8,128)S(1)}, f32[16,8,128]{2,1,0:T(8,128)S(1)}, bf16[2048,1024]{1,0:T(8,128)(2,1)S(1)}) custom-call(bf16[2048,1024]{1,0:T(8,128)(2,1)} %docs_hbm, bf16[1024,1024]{1,0:T(8,128)(2,1)} %cent_hbm.1), custom_call_target="tpu_custom_call" | custom-call | tf_op jit(solution)/shard_map/first/pallas_call | solution.py:110
  9.4 13.9 %all_to_all.35.got_ref = f32[16,8,128]{2,1,0:T(8,128)S(1)} all-to-all(f32[16,8,128]{2,1,0:T(8,128)S(1)} %get-tuple-element.17), channel_id=1, replica_groups=mesh['x'=4,'z'=8,'c'=2,'y'=4] {'x','y'}, dimensions={0} | all-to-all | bytes 131072 | tf_op jit(solution)/shard_map/all_to_all | solution.py:337
  23.3 18.1 %all_to_all.36.got_ref = f32[16,8,128]{2,1,0:T(8,128)S(1)} all-to-all(f32[16,8,128]{2,1,0:T(8,128)S(1)} %sum.2), channel_id=1, replica_groups=mesh['x'=4,'z'=8,'c'=2,'y'=4] {'z','c'}, dimensions={0} | all-to-all | bytes 131072 | tf_op jit(solution)/shard_map/all_to_all | solution.py:338
  41.5 0.0 copy-done
  41.5 3.4 %middle.1 = f32[16,8,128]{2,1,0:T(8,128)S(1)} custom-call(f32[4,1024,512]{2,1,0:T(8,128)S(1)} %get-tuple-element.16.scores_ref, f32[16,8,128]{2,1,0:T(8,128)S(1)} %all_to_all.36.got_ref, f32[8,128]{1,0:T(8,128)S(1)} %bitcast.7), custom_call_target="tpu_custom_call" | custom-call | tf_op jit(solution)/shard_map/middle/pallas_call | solution.py:143
  45.0 9.5 %all_to_all.37.got_ref = f32[16,8,128]{2,1,0:T(8,128)S(1)} all-to-all(f32[16,8,128]{2,1,0:T(8,128)S(1)} %middle.1), channel_id=1, replica_groups=mesh['x'=4,'z'=8,'c'=2,'y'=4] {'x','y'}, dimensions={0} | all-to-all | bytes 131072 | tf_op jit(solution)/shard_map/all_to_all | solution.py:337
  54.4 11.8 %all_to_all.38.got_ref = f32[16,8,128]{2,1,0:T(8,128)S(1)} all-to-all(f32[16,8,128]{2,1,0:T(8,128)S(1)} %sum.3), channel_id=1, replica_groups=mesh['x'=4,'z'=8,'c'=2,'y'=4] {'z','c'}, dimensions={0} | all-to-all | bytes 131072 | tf_op jit(solution)/shard_map/all_to_all | solution.py:338
  66.2 7.8 %last.1 = (bf16[1024,512]{1,0:T(8,128)(2,1)S(1)}, f32[1024,512]{1,0:T(8,128)S(1)}, f32[1,8,128]{2,1,0:T(8,128)S(1)}) custom-call(s32[1]{0:T(128)} %bitcast.core_ref, f32[4,1024,512]{2,1,0:T(8,128)S(1)} %get-tuple-element.16.scores_ref, f32[16,8,128]{2,1,0:T(8,128)S(1)} %all_to_all.38.got_ref, f32[8,128]{1,0:T(8,128)S(1)} %bitcast.8, ...), custom_call_target="tpu_custom_call" | custom-call | tf_op jit(solution)/shard_map/last/pallas_call | solution.py:185
  74.0 0.2 collective-permute-start
  74.2 0.4 collective-permute-start.1
  74.6 2.2 %collective-permute-done.1.mass_got_ref = f32[1,8,128]{2,1,0:T(8,128)S(1)} collective-permute-done((f32[1,8,128]{2,1,0:T(8,128)S(1)}, f32[1,8,128]{2,1,0:T(8,128)S(1)}, u32[]{:S(2)}, u32[]{:S(2)}) %collective-permute-start.1) | collective-permute-done | bytes 4128 | tf_op jit(solution)/shard_map/ppermute | solution.py:26
  76.7 0.0 collective-permute-done.got_ref
  76.7 0.3 pack.1
  77.0 21.2 %all_to_all.39.got_ref = bf16[16,72,512]{2,1,0:T(8,128)(2,1)S(1)} all-to-all(bf16[16,72,512]{2,1,0:T(8,128)(2,1)S(1)} %pack.1), channel_id=1, replica_groups=mesh['x'=4,'z'=8,'c'=2,'y'=4] {'y','x'}, dimensions={0} | all-to-all | bytes 2359296 | tf_op jit(solution)/shard_map/all_to_all | solution.py:356
  98.2 0.2 repack.1
  98.3 12.6 %all_to_all.40.got_ref = f32[8,16,512]{2,1,0:T(8,128)S(1)} all-to-all(f32[8,16,512]{2,1,0:T(8,128)S(1)} %repack.1), channel_id=1, replica_groups=mesh['x'=4,'z'=8,'c'=2,'y'=4] {'z'}, dimensions={0} | all-to-all | bytes 524288 | tf_op jit(solution)/shard_map/all_to_all | solution.py:357
  110.9 0.6 finish.1
  111.5 13.1 %all_to_all.41 = bf16[32,8,512]{2,1,0:T(8,128)(2,1)S(1)} all-to-all(bf16[32,8,512]{2,1,0:T(8,128)(2,1)S(1)} %get-tuple-element.22), channel_id=1, replica_groups=mesh['x'=4,'z'=8,'c'=2,'y'=4] {'x','z'}, dimensions={0} | all-to-all | bytes 524288 | tf_op jit(solution)/shard_map/all_to_all | solution.py:359
  124.7 3.8 %collective-permute-start.2 = (bf16[256,512]{1,0:T(8,128)(2,1)S(1)}, bf16[256,512]{1,0:T(8,128)(2,1)S(1)}, u32[]{:S(2)}, u32[]{:S(2)}) collective-permute-start(bf16[256,512]{1,0:T(8,128)(2,1)S(1)} %bitcast.5), channel_id=1, source_target_pairs={{0,4},{4,0},{1,5},{5,1},{2,6},{6,2},{3,7},{7,3},{8,12},{12,8},{9,1... | collective-permute-start | bytes 786440 | tf_op jit(solution)/shard_map/ppermute | solution.py:26
  128.4 1.2 collective-permute-done.2.other_ref
  129.6 0.8 join.1
  (2 shorter events, 0.0 us)
Async XLA Ops:
  0.6 40.9 %copy-start = (f32[1024]{0:T(1024)S(1)}, f32[1024]{0:T(1024)}, u32[]{:S(2)}) copy-start(f32[1024]{0:T(1024)} %param.5) | copy-start | bytes 12292
  74.0 2.8 %collective-permute-start = (bf16[1024,512]{1,0:T(8,128)(2,1)S(1)}, bf16[1024,512]{1,0:T(8,128)(2,1)S(1)}, u32[]{:S(2)}, u32[]{:S(2)}) collective-permute-start(bf16[1024,512]{1,0:T(8,128)(2,1)S(1)} %get-tuple-element.20), channel_id=1, source_target_pairs={{0,4},{4,0},{1,5},{5,1},{2,6},{6,2},{3,7},{7,3},{8,12},{12,8},{9,1... | collective-permute-start | bytes 3145736 | tf_op jit(solution)/shard_map/ppermute | solution.py:26
  74.2 2.5 %collective-permute-start.1 = (f32[1,8,128]{2,1,0:T(8,128)S(1)}, f32[1,8,128]{2,1,0:T(8,128)S(1)}, u32[]{:S(2)}, u32[]{:S(2)}) collective-permute-start(f32[1,8,128]{2,1,0:T(8,128)S(1)} %get-tuple-element.21.mass_ref), channel_id=1, source_target_pairs={{0,4},{4,0},{1,5},{5,1},{2,6},{6,2},{3,7},{7,3},{8,12},{12,8},{9,1... | collective-permute-start | bytes 12296 | tf_op jit(solution)/shard_map/ppermute | solution.py:26
  124.7 4.9 %collective-permute-start.2 = (bf16[256,512]{1,0:T(8,128)(2,1)S(1)}, bf16[256,512]{1,0:T(8,128)(2,1)S(1)}, u32[]{:S(2)}, u32[]{:S(2)}) collective-permute-start(bf16[256,512]{1,0:T(8,128)(2,1)S(1)} %bitcast.5), channel_id=1, source_target_pairs={{0,4},{4,0},{1,5},{5,1},{2,6},{6,2},{3,7},{7,3},{8,12},{12,8},{9,1... | collective-permute-start | bytes 786440 | tf_op jit(solution)/shard_map/ppermute | solution.py:26

commit v4 on v3

--- a/solution.py
+++ b/solution.py
@@ -18,7 +18,6 @@
 BLOCK = 512
 CHUNK = 64
 LOG2E = 1 / math.log(2)
-TILE = 256
 MIB = 2**20
 
 
@@ -84,13 +83,16 @@
     for block in range(n_blocks):
         rows = pl.ds(block * BLOCK, BLOCK)
         copies.append(pltpu.make_async_copy(docs_hbm.at[rows], docs_ref.at[rows], sems.at[block]))
-    for copy in copies:
-        copy.start()
+    copies[0].start()
+    copies[1].start()
     acc[...] = jnp.zeros_like(acc)
     copies[0].wait()
     for block in range(n_blocks + 1):
         if block < n_blocks:
             copies[block + 1].wait()
+            if block == 0:
+                for copy in copies[2:]:
+                    copy.start()
             scores_ref[block] = lax.dot_general(
                 cent_ref[...],
                 docs_ref[block * BLOCK : (block + 1) * BLOCK, :],
@@ -154,27 +156,35 @@
     )(scores, got, cluster_mass)
 
 
-def last_kernel(loga, core_ref, scores_ref, got_ref, cluster_mass_ref, docs_ref, send_ref, own_ref, mass_ref, plan, duals_col, acc):
+def half_columns(core, half):
+    return pl.ds(pl.multiple_of(core * half, half), half)
+
+
+def last_kernel(loga, core_ref, scores_ref, got_ref, cluster_mass_ref, docs_ref, send_ref, plan_ref, mass_ref, total, duals_col, acc):
+    n_blocks = scores_ref.shape[0]
+    columns = half_columns(1 - core_ref[0], send_ref.shape[1])
     start_duals(got_ref, cluster_mass_ref, duals_col)
     acc[...] = jnp.zeros_like(acc)
-
-    @pl.loop(0, scores_ref.shape[0])
-    def _(block):
-        def emit(row, mass):
-            add_lanes(acc, row, mass)
-            columns = pl.ds(pl.multiple_of(block * BLOCK, BLOCK), BLOCK)
-            plan[row : row + CHUNK, columns] = mass.astype(jnp.bfloat16)
-
-        block_masses(scores_ref.at[block], slice(0, BLOCK), duals_col, loga, emit)
-
+    for block in range(n_blocks + 1):
+        if block > 0:
+            rows = slice((block - 1) * BLOCK, block * BLOCK)
+            part = lax.dot_general(
+                plan_ref[:, rows], docs_ref[rows, columns], (((1,), (0,)), ((), ())), preferred_element_type=jnp.float32
+            )
+            if block > 1:
+                part += total[...]
+            if block < n_blocks:
+                total[...] = part
+            else:
+                send_ref[...] = part.astype(jnp.bfloat16)
+        if block < n_blocks:
+
+            def emit(row, mass, start=block * BLOCK):
+                add_lanes(acc, row, mass)
+                plan_ref[row : row + CHUNK, start : start + BLOCK] = mass.astype(jnp.bfloat16)
+
+            block_masses(scores_ref.at[block], slice(0, BLOCK), duals_col, loga, emit)
     column_sums(acc, mass_ref)
-    half = own_ref.shape[1]
-    for out_ref, owner in ((send_ref, 1 - core_ref[0]), (own_ref, core_ref[0])):
-        for tile in range(0, half, TILE):
-            columns = pl.ds(pl.multiple_of(owner * half + tile, TILE), TILE)
-            out_ref[:, tile : tile + TILE] = lax.dot_general(
-                plan[...], docs_ref[:, columns], (((1,), (0,)), ((), ())), preferred_element_type=jnp.float32
-            ).astype(out_ref.dtype)
 
 
 def last_call(scores, got, cluster_mass, documents, core, loga):
@@ -188,17 +198,44 @@
         out_specs=[vmem] * 3,
         out_shape=[
             pltpu.VMEM((n_clusters, half), jnp.bfloat16),
+            pltpu.VMEM((n_clusters, n_docs), jnp.bfloat16),
+            pltpu.VMEM((1, n_clusters // LANES, LANES), jnp.float32),
+        ],
+        scratch_shapes=[
             pltpu.VMEM((n_clusters, half), jnp.float32),
-            pltpu.VMEM((1, n_clusters // LANES, LANES), jnp.float32),
-        ],
-        scratch_shapes=[
-            pltpu.VMEM((n_clusters, n_docs), jnp.bfloat16),
             pltpu.VMEM((n_clusters, LANES), jnp.float32),
             pltpu.VMEM((n_clusters, LANES), jnp.float32),
         ],
-        compiler_params=pltpu.CompilerParams(vmem_limit_bytes=20 * MIB),
+        compiler_params=pltpu.CompilerParams(vmem_limit_bytes=16 * MIB),
         name="last",
     )(core, scores, got, cluster_mass, documents)
+
+
+def own_kernel(core_ref, plan_ref, docs_ref, own_ref):
+    half = own_ref.shape[1]
+    own_ref[...] = lax.dot_general(
+        plan_ref[...],
+        docs_ref[:, half_columns(core_ref[0], half)],
+        (((1,), (0,)), ((), ())),
+        preferred_element_type=jnp.float32,
+    )
+
+
+def own_call(plan, documents, core):
+    n_clusters, n_docs = plan.shape
+    half = documents.shape[1] // NC
+    vmem = pl.BlockSpec(memory_space=pltpu.VMEM)
+    return pl.pallas_call(
+        own_kernel,
+        in_specs=[pl.BlockSpec(memory_space=pltpu.SMEM), vmem, vmem],
+        out_specs=vmem,
+        out_shape=pltpu.VMEM((n_clusters, half), jnp.float32),
+        compiler_params=pltpu.CompilerParams(vmem_limit_bytes=8 * MIB),
+        cost_estimate=pl.CostEstimate(
+            flops=2 * n_clusters * n_docs * half, bytes_accessed=2 * n_docs * (n_clusters + half), transcendentals=0
+        ),
+        name="own",
+    )(core, plan, documents)
 
 
 def sum_kernel(got_ref, out_ref):
@@ -256,33 +293,31 @@
     total = got_ref[0].astype(jnp.float32)
     for k in range(1, got_ref.shape[0]):
         total += got_ref[k].astype(jnp.float32)
-    extra = total[slab:]
-    extra = extra + jnp.concatenate([extra[:, LANES:], extra[:, :LANES]], axis=1) + jnp.concatenate(
-        [extra[:, 2 * LANES :], extra[:, : 2 * LANES]], axis=1
-    )
+    half = total.shape[1]
+    mass = total[slab:, :LANES] + total[slab:, LANES : 2 * LANES] + total[slab:, 2 * LANES : 3 * LANES]
     for k in range(NZ):
-        out_ref[k, :rows, :] = total[k * rows : (k + 1) * rows]
-        out_ref[k, rows:, :] = extra
+        out_ref[k, :, :half] = total[k * rows : (k + 1) * rows]
+        out_ref[k, :, half:] = mass
 
 
 def repack_call(got, slab):
     vmem = pl.BlockSpec(memory_space=pltpu.VMEM)
-    shape = (NZ, slab // NZ + got.shape[1] - slab, got.shape[2])
     return pl.pallas_call(
         functools.partial(repack_kernel, slab),
         in_specs=[vmem],
         out_specs=vmem,
-        out_shape=pltpu.VMEM(shape, jnp.float32),
+        out_shape=pltpu.VMEM((NZ, slab // NZ, got.shape[2] + LANES), jnp.float32),
         compiler_params=pltpu.CompilerParams(vmem_limit_bytes=8 * MIB),
         name="repack",
     )(got)
 
 
-def finish_kernel(rows, place_ref, got_ref, cluster_mass_ref, out_ref, duals_ref):
+def finish_kernel(place_ref, got_ref, cluster_mass_ref, out_ref, duals_ref):
     total = got_ref[0]
     for k in range(1, got_ref.shape[0]):
         total += got_ref[k]
-    mass = total[rows:, :LANES]
+    half = out_ref.shape[2]
+    mass = total[:, half:]
     duals_ref[...] = TAU * (jnp.log(cluster_mass_ref[...]) - jnp.log(mass))
     place = place_ref[0]
     group = place // LANES
@@ -292,16 +327,16 @@
     line = jnp.sum(jnp.where(row == group, mass, 0.0), axis=0, keepdims=True)
     mine = jnp.where(lane == row + first, jnp.broadcast_to(line, mass.shape), 0.0)
     own_mass = jnp.sum(mine, axis=1, keepdims=True)
-    centroids = (total[:rows] / own_mass).astype(jnp.bfloat16)
+    centroids = (total[:, :half] / own_mass).astype(jnp.bfloat16)
     for k in range(out_ref.shape[0]):
         out_ref[k] = centroids
 
 
-def finish_call(got, cluster_mass, place, rows):
-    half = got.shape[2]
-    vmem = pl.BlockSpec(memory_space=pltpu.VMEM)
-    return pl.pallas_call(
-        functools.partial(finish_kernel, rows),
+def finish_call(got, cluster_mass, place):
+    rows, half = got.shape[1], got.shape[2] - LANES
+    vmem = pl.BlockSpec(memory_space=pltpu.VMEM)
+    return pl.pallas_call(
+        finish_kernel,
         in_specs=[pl.BlockSpec(memory_space=pltpu.SMEM), vmem, vmem],
         out_specs=[vmem, vmem],
         out_shape=[
@@ -351,11 +386,12 @@
     cluster_mass = cluster_mass.reshape(n_clusters // LANES, LANES)
     scores, mass, documents = first_call(documents, centroids, loga)
     mass = middle_call(scores, sum_all(mass), cluster_mass, loga)
-    send, own, mass = last_call(scores, sum_all(mass), cluster_mass, documents, core, loga)
+    send, plan, mass = last_call(scores, sum_all(mass), cluster_mass, documents, core, loga)
+    own = own_call(plan, documents, core)
     packed = pack_call(own, swap_cores(send), mass, swap_cores(mass))
     packed = repack_call(lax.all_to_all(packed, ("y", "x"), 0, 0, tiled=True), slab)
     packed = lax.all_to_all(packed, ("z",), 0, 0, tiled=True)
-    mine, duals = finish_call(packed, cluster_mass, place, rows)
+    mine, duals = finish_call(packed, cluster_mass, place)
     block = lax.all_to_all(mine, ("x", "z"), 0, 0, tiled=True).reshape(n_clusters // NY, half)
     return join_call(core, block, swap_cores(block)), duals.reshape(n_clusters)
 

time: 131 us -> 126 us (0.962)
  blocking collectives: 100 us -> 97.5 us
  waiting for transfers between devices: 3.32 us -> 1.17 us
    pallas_call x1, Pallas kernels: 7.76 us -> 4.99 us  [last_call(): pl.pallas_call(functools.partial(last_kernel, loga), in_specs=[pl.BlockSp...]
    pallas_call x1 -> x2, Pallas kernels: 0.61 us -> 2.93 us  [the longest x1 2.32 us: own_call(): pl.pallas_call(own_kernel, in_specs=[pl.BlockSpec(memory_space=pltpu.SMEM...]
    ppermute x3, waiting for transfers between devices: 3.32 us -> 1.17 us  [swap_cores(): return lax.ppermute(value, 'c', [(0, 1), (1, 0)])]
    all_to_all x1, blocking collectives: 12.6 us -> 10.4 us  [per_device(): packed = lax.all_to_all(packed, ('z',), 0, 0, tiled=True)]
  transfers between devices with their start and end apart: 3 -> 3, of which waited for: 2 -> 1; matrix products, arithmetic and copies ran while one was open for 0% -> 0% of each run, Pallas kernels for 0% -> 2%
where the time goes in v4:
time: 126 us
  blocking collectives  97.5 us (77%)
  Pallas kernels  21.4 us (17%)
  starting transfers between devices  4.79 us (4%)
    all_to_all x2, blocking collectives, sum_all(): return lax.all_to_all(sum_call(got, NZ * NC), ('z', 'c'), 0, 0, tiled=True)  29.9 us
    all_to_all x2, blocking collectives, sum_all(): got = lax.all_to_all(copies, ('x', 'y'), 0, 0, tiled=True)  23.3 us
    all_to_all x1, blocking collectives, per_device(): lax.all_to_all(packed, ('y', 'x'), 0, 0, tiled=True)  21.1 us
    all_to_all x1, blocking collectives, per_device(): lax.all_to_all(mine, ('x', 'z'), 0, 0, tiled=True)  12.6 us
    all_to_all x1, blocking collectives, per_device(): packed = lax.all_to_all(packed, ('z',), 0, 0, tiled=True)  10.4 us
    pallas_call x1, Pallas kernels, first_call(): pl.pallas_call(functools.partial(first_kernel, loga), in_specs=[pl.BlockS...  8.78 us
    pallas_call x1, Pallas kernels, last_call(): pl.pallas_call(functools.partial(last_kernel, loga), in_specs=[pl.BlockSp...  4.99 us
    ppermute x3, starting transfers between devices, swap_cores(): return lax.ppermute(value, 'c', [(0, 1), (1, 0)])  4.79 us
  transfers between devices with their start and end apart: 3, of which 1 were waited for; matrix products, arithmetic and copies ran while one was open for 0% of the time, Pallas kernels for 2%

profile of v4, /device:TPU:1, one launch (start us, length us, event | category | flops | bytes accessed | tf_op | source)
XLA Modules:
  0.0 125.5 jit_solution(9725297216029938587)
XLA Ops:
  0.6 0.0 copy-start
  0.7 8.8 %first.1 = (f32[4,1024,512]{2,1,0:T(8,128)S(1)}, f32[16,8,128]{2,1,0:T(8,128)S(1)}, bf16[2048,1024]{1,0:T(8,128)(2,1)S(1)}) custom-call(bf16[2048,1024]{1,0:T(8,128)(2,1)} %docs_hbm, bf16[1024,1024]{1,0:T(8,128)(2,1)} %cent_hbm.1), custom_call_target="tpu_custom_call" | custom-call | tf_op jit(solution)/shard_map/first/pallas_call | solution.py:112
  9.4 13.9 %all_to_all.35.got_ref = f32[16,8,128]{2,1,0:T(8,128)S(1)} all-to-all(f32[16,8,128]{2,1,0:T(8,128)S(1)} %get-tuple-element.17), channel_id=1, replica_groups=mesh['x'=4,'z'=8,'c'=2,'y'=4] {'x','y'}, dimensions={0} | all-to-all | bytes 131072 | tf_op jit(solution)/shard_map/all_to_all | solution.py:372
  23.3 18.2 %all_to_all.36.got_ref = f32[16,8,128]{2,1,0:T(8,128)S(1)} all-to-all(f32[16,8,128]{2,1,0:T(8,128)S(1)} %sum.2), channel_id=1, replica_groups=mesh['x'=4,'z'=8,'c'=2,'y'=4] {'z','c'}, dimensions={0} | all-to-all | bytes 131072 | tf_op jit(solution)/shard_map/all_to_all | solution.py:373
  41.5 0.0 copy-done
  41.5 3.4 %middle.1 = f32[16,8,128]{2,1,0:T(8,128)S(1)} custom-call(f32[4,1024,512]{2,1,0:T(8,128)S(1)} %get-tuple-element.16.scores_ref, f32[16,8,128]{2,1,0:T(8,128)S(1)} %all_to_all.36.got_ref, f32[8,128]{1,0:T(8,128)S(1)} %bitcast.7), custom_call_target="tpu_custom_call" | custom-call | tf_op jit(solution)/shard_map/middle/pallas_call | solution.py:145
  45.0 9.5 %all_to_all.37.got_ref = f32[16,8,128]{2,1,0:T(8,128)S(1)} all-to-all(f32[16,8,128]{2,1,0:T(8,128)S(1)} %middle.1), channel_id=1, replica_groups=mesh['x'=4,'z'=8,'c'=2,'y'=4] {'x','y'}, dimensions={0} | all-to-all | bytes 131072 | tf_op jit(solution)/shard_map/all_to_all | solution.py:372
  54.4 11.8 %all_to_all.38.got_ref = f32[16,8,128]{2,1,0:T(8,128)S(1)} all-to-all(f32[16,8,128]{2,1,0:T(8,128)S(1)} %sum.3), channel_id=1, replica_groups=mesh['x'=4,'z'=8,'c'=2,'y'=4] {'z','c'}, dimensions={0} | all-to-all | bytes 131072 | tf_op jit(solution)/shard_map/all_to_all | solution.py:373
  66.2 5.0 %last.1 = (bf16[1024,512]{1,0:T(8,128)(2,1)S(1)}, bf16[1024,2048]{1,0:T(8,128)(2,1)S(1)}, f32[1,8,128]{2,1,0:T(8,128)S(1)}) custom-call(s32[1]{0:T(128)} %bitcast.core_ref, f32[4,1024,512]{2,1,0:T(8,128)S(1)} %get-tuple-element.16.scores_ref, f32[16,8,128]{2,1,0:T(8,128)S(1)} %all_to_all.38.got_ref, f32[8,128]{1,0:T(8,128)S(1)} %bitcast.8, ...), custom_call_target="tpu_custom_call" | custom-call | tf_op jit(solution)/shard_map/last/pallas_call | solution.py:195
  71.2 0.3 collective-permute-start
  71.5 0.3 collective-permute-start.1
  71.8 2.3 %own.1.own_ref = f32[1024,512]{1,0:T(8,128)S(1)} custom-call(s32[1]{0:T(128)} %bitcast.core_ref, bf16[1024,2048]{1,0:T(8,128)(2,1)S(1)} %get-tuple-element.19.plan_ref, bf16[2048,1024]{1,0:T(8,128)(2,1)S(1)} %get-tuple-element.18.docs_ref), custom_call_target="tpu_custom_call" | custom-call | flops 2147483648 | bytes 6291456 | tf_op jit(solution)/shard_map/own/pallas_call | solution.py:228
  74.1 0.0 collective-permute-done.1.mass_got_ref
  74.1 0.0 collective-permute-done.got_ref
  74.1 0.2 pack.1
  74.4 21.1 %all_to_all.39.got_ref = bf16[16,72,512]{2,1,0:T(8,128)(2,1)S(1)} all-to-all(bf16[16,72,512]{2,1,0:T(8,128)(2,1)S(1)} %pack.1), channel_id=1, replica_groups=mesh['x'=4,'z'=8,'c'=2,'y'=4] {'y','x'}, dimensions={0} | all-to-all | bytes 2359296 | tf_op jit(solution)/shard_map/all_to_all | solution.py:392
  95.5 0.2 repack.1
  95.7 10.4 %all_to_all.40.got_ref = f32[8,8,640]{2,1,0:T(8,128)S(1)} all-to-all(f32[8,8,640]{2,1,0:T(8,128)S(1)} %repack.1), channel_id=1, replica_groups=mesh['x'=4,'z'=8,'c'=2,'y'=4] {'z'}, dimensions={0} | all-to-all | bytes 327680 | tf_op jit(solution)/shard_map/all_to_all | solution.py:393
  106.1 0.6 finish.1
  106.7 12.6 %all_to_all.41 = bf16[32,8,512]{2,1,0:T(8,128)(2,1)S(1)} all-to-all(bf16[32,8,512]{2,1,0:T(8,128)(2,1)S(1)} %get-tuple-element.22), channel_id=1, replica_groups=mesh['x'=4,'z'=8,'c'=2,'y'=4] {'x','z'}, dimensions={0} | all-to-all | bytes 524288 | tf_op jit(solution)/shard_map/all_to_all | solution.py:395
  119.3 4.2 %collective-permute-start.2 = (bf16[256,512]{1,0:T(8,128)(2,1)S(1)}, bf16[256,512]{1,0:T(8,128)(2,1)S(1)}, u32[]{:S(2)}, u32[]{:S(2)}) collective-permute-start(bf16[256,512]{1,0:T(8,128)(2,1)S(1)} %bitcast.5), channel_id=1, source_target_pairs={{0,4},{4,0},{1,5},{5,1},{2,6},{6,2},{3,7},{7,3},{8,12},{12,8},{9,1... | collective-permute-start | bytes 786440 | tf_op jit(solution)/shard_map/ppermute | solution.py:25
  123.5 1.2 collective-permute-done.2.other_ref
  124.7 0.8 join.1
  (2 shorter events, 0.0 us)
Async XLA Ops:
  0.6 40.9 %copy-start = (f32[1024]{0:T(1024)S(1)}, f32[1024]{0:T(1024)}, u32[]{:S(2)}) copy-start(f32[1024]{0:T(1024)} %param.5) | copy-start | bytes 12292
  71.2 2.9 %collective-permute-start = (bf16[1024,512]{1,0:T(8,128)(2,1)S(1)}, bf16[1024,512]{1,0:T(8,128)(2,1)S(1)}, u32[]{:S(2)}, u32[]{:S(2)}) collective-permute-start(bf16[1024,512]{1,0:T(8,128)(2,1)S(1)} %get-tuple-element.20), channel_id=1, source_target_pairs={{0,4},{4,0},{1,5},{5,1},{2,6},{6,2},{3,7},{7,3},{8,12},{12,8},{9,1... | collective-permute-start | bytes 3145736 | tf_op jit(solution)/shard_map/ppermute | solution.py:25
  71.5 2.7 %collective-permute-start.1 = (f32[1,8,128]{2,1,0:T(8,128)S(1)}, f32[1,8,128]{2,1,0:T(8,128)S(1)}, u32[]{:S(2)}, u32[]{:S(2)}) collective-permute-start(f32[1,8,128]{2,1,0:T(8,128)S(1)} %get-tuple-element.21.mass_ref), channel_id=1, source_target_pairs={{0,4},{4,0},{1,5},{5,1},{2,6},{6,2},{3,7},{7,3},{8,12},{12,8},{9,1... | collective-permute-start | bytes 12296 | tf_op jit(solution)/shard_map/ppermute | solution.py:25
  119.3 5.4 %collective-permute-start.2 = (bf16[256,512]{1,0:T(8,128)(2,1)S(1)}, bf16[256,512]{1,0:T(8,128)(2,1)S(1)}, u32[]{:S(2)}, u32[]{:S(2)}) collective-permute-start(bf16[256,512]{1,0:T(8,128)(2,1)S(1)} %bitcast.5), channel_id=1, source_target_pairs={{0,4},{4,0},{1,5},{5,1},{2,6},{6,2},{3,7},{7,3},{8,12},{12,8},{9,1... | collective-permute-start | bytes 786440 | tf_op jit(solution)/shard_map/ppermute | solution.py:25

commit v5 on v4

--- a/solution.py
+++ b/solution.py
@@ -16,6 +16,7 @@
 AXES = ("x", "z", "c", "y")
 LANES = 128
 BLOCK = 512
+GROUP = 2
 CHUNK = 64
 LOG2E = 1 / math.log(2)
 MIB = 2**20
@@ -62,15 +63,20 @@
 
 def column_sums(acc, out_ref):
     rows = [jnp.sum(acc[k : k + LANES, :].T, axis=0, keepdims=True) for k in range(0, acc.shape[0], LANES)]
-    sums = jnp.concatenate(rows, axis=0)
+    sums = jnp.concatenate(rows, axis=0).astype(out_ref.dtype)
     for slot in range(out_ref.shape[0]):
         out_ref[slot] = sums
 
 
+def sum_slots(got_ref):
+    total = got_ref[0].astype(jnp.float32)
+    for slot in range(1, got_ref.shape[0]):
+        total += got_ref[slot].astype(jnp.float32)
+    return total
+
+
 def start_duals(got_ref, cluster_mass_ref, duals_col):
-    column_mass = got_ref[0]
-    for slot in range(1, got_ref.shape[0]):
-        column_mass += got_ref[slot]
+    column_mass = sum_slots(got_ref)
     duals = TAU * (jnp.log2(cluster_mass_ref[...]) - jnp.log2(column_mass))
     for k in range(duals.shape[0]):
         row = jnp.broadcast_to(duals[k : k + 1, :], (LANES, LANES))
@@ -83,22 +89,25 @@
     for block in range(n_blocks):
         rows = pl.ds(block * BLOCK, BLOCK)
         copies.append(pltpu.make_async_copy(docs_hbm.at[rows], docs_ref.at[rows], sems.at[block]))
-    copies[0].start()
-    copies[1].start()
+    for copy in copies[: 1 + GROUP]:
+        copy.start()
     acc[...] = jnp.zeros_like(acc)
     copies[0].wait()
     for block in range(n_blocks + 1):
-        if block < n_blocks:
-            copies[block + 1].wait()
+        if block % GROUP == 0 and block < n_blocks:
+            for k in range(block, block + GROUP):
+                copies[k + 1].wait()
             if block == 0:
-                for copy in copies[2:]:
+                for copy in copies[1 + GROUP :]:
                     copy.start()
-            scores_ref[block] = lax.dot_general(
+            scores = lax.dot_general(
                 cent_ref[...],
-                docs_ref[block * BLOCK : (block + 1) * BLOCK, :],
+                docs_ref[block * BLOCK : (block + GROUP) * BLOCK, :],
                 (((1,), (1,)), ((), ())),
                 preferred_element_type=jnp.float32,
             ) * (TEMP / math.sqrt(D) * LOG2E)
+            for k in range(GROUP):
+                scores_ref[block + k] = scores[:, k * BLOCK : (k + 1) * BLOCK]
         if block > 0:
             block_masses(scores_ref.at[block - 1], slice(0, BLOCK), None, loga, functools.partial(add_lanes, acc))
     column_sums(acc, mass_ref)
@@ -115,7 +124,7 @@
         out_specs=[vmem] * 3,
         out_shape=[
             pltpu.VMEM((n_blocks, n_clusters, BLOCK), jnp.float32),
-            pltpu.VMEM((NX * NY, n_clusters // LANES, LANES), jnp.float32),
+            pltpu.VMEM((NX * NY, n_clusters // LANES, LANES), jnp.bfloat16),
             pltpu.VMEM((n_docs, dim), jnp.bfloat16),
         ],
         scratch_shapes=[
@@ -146,7 +155,7 @@
         functools.partial(middle_kernel, loga),
         in_specs=[vmem] * 3,
         out_specs=vmem,
-        out_shape=pltpu.VMEM((NX * NY, n_clusters // LANES, LANES), jnp.float32),
+        out_shape=pltpu.VMEM((NX * NY, n_clusters // LANES, LANES), jnp.bfloat16),
         scratch_shapes=[
             pltpu.VMEM((n_clusters, LANES), jnp.float32),
             pltpu.VMEM((n_clusters, LANES), jnp.float32),
@@ -239,9 +248,7 @@
 
 
 def sum_kernel(got_ref, out_ref):
-    total = got_ref[0]
-    for slot in range(1, got_ref.shape[0]):
-        total += got_ref[slot]
+    total = sum_slots(got_ref).astype(out_ref.dtype)
     for slot in range(out_ref.shape[0]):
         out_ref[slot] = total
 
@@ -259,63 +266,63 @@
 
 
 def pack_kernel(own_ref, got_ref, mass_ref, mass_got_ref, out_ref):
-    half = own_ref.shape[1]
     n_slabs = out_ref.shape[0]
     slab = own_ref.shape[0] // n_slabs
     mass = mass_ref[0] + mass_got_ref[0]
     high = mass.astype(jnp.bfloat16)
-    middle = (mass - high.astype(jnp.float32)).astype(jnp.bfloat16)
-    low = (mass - high.astype(jnp.float32) - middle.astype(jnp.float32)).astype(jnp.bfloat16)
-    rest = jnp.zeros((mass.shape[0], half - 3 * LANES), jnp.bfloat16)
-    extra = jnp.concatenate([high, middle, low, rest], axis=1)
+    low = (mass - high.astype(jnp.float32)).astype(jnp.bfloat16)
     for k in range(n_slabs):
         rows = slice(k * slab, (k + 1) * slab)
-        out_ref[k, :slab, :] = (own_ref[rows, :] + got_ref[rows, :].astype(jnp.float32)).astype(jnp.bfloat16)
-        out_ref[k, slab:, :] = extra
+        total = (own_ref[rows, :] + got_ref[rows, :].astype(jnp.float32)).astype(jnp.bfloat16)
+        pieces = [total[:, lane : lane + LANES] for lane in range(0, own_ref.shape[1], LANES)] + [high, low]
+        first = 0
+        for piece in pieces:
+            out_ref[k, first : first + piece.shape[0], :] = piece
+            first += piece.shape[0]
 
 
 def pack_call(own, got, mass, mass_got):
     n_clusters, half = own.shape
     n_slabs = NX * NY
+    rows = n_clusters // n_slabs * (half // LANES) + 2 * mass.shape[1]
     vmem = pl.BlockSpec(memory_space=pltpu.VMEM)
     return pl.pallas_call(
         pack_kernel,
         in_specs=[vmem] * 4,
         out_specs=vmem,
-        out_shape=pltpu.VMEM((n_slabs, n_clusters // n_slabs + mass.shape[1], half), jnp.bfloat16),
+        out_shape=pltpu.VMEM((n_slabs, rows, LANES), jnp.bfloat16),
         compiler_params=pltpu.CompilerParams(vmem_limit_bytes=8 * MIB),
         name="pack",
     )(own, got, mass, mass_got)
 
 
 def repack_kernel(slab, got_ref, out_ref):
+    groups = out_ref.shape[2] // LANES - 1
     rows = slab // NZ
-    total = got_ref[0].astype(jnp.float32)
-    for k in range(1, got_ref.shape[0]):
-        total += got_ref[k].astype(jnp.float32)
-    half = total.shape[1]
-    mass = total[slab:, :LANES] + total[slab:, LANES : 2 * LANES] + total[slab:, 2 * LANES : 3 * LANES]
+    total = sum_slots(got_ref)
+    mass = total[groups * slab : groups * slab + 8] + total[groups * slab + 8 :]
     for k in range(NZ):
-        out_ref[k, :, :half] = total[k * rows : (k + 1) * rows]
-        out_ref[k, :, half:] = mass
+        for group in range(groups):
+            first = group * slab + k * rows
+            out_ref[k, :, group * LANES : (group + 1) * LANES] = total[first : first + rows]
+        out_ref[k, :, groups * LANES :] = mass
 
 
 def repack_call(got, slab):
+    groups = (got.shape[1] - 16) // slab
     vmem = pl.BlockSpec(memory_space=pltpu.VMEM)
     return pl.pallas_call(
         functools.partial(repack_kernel, slab),
         in_specs=[vmem],
         out_specs=vmem,
-        out_shape=pltpu.VMEM((NZ, slab // NZ, got.shape[2] + LANES), jnp.float32),
+        out_shape=pltpu.VMEM((NZ, slab // NZ, (groups + 1) * LANES), jnp.float32),
         compiler_params=pltpu.CompilerParams(vmem_limit_bytes=8 * MIB),
         name="repack",
     )(got)
 
 
 def finish_kernel(place_ref, got_ref, cluster_mass_ref, out_ref, duals_ref):
-    total = got_ref[0]
-    for k in range(1, got_ref.shape[0]):
-        total += got_ref[k]
+    total = sum_slots(got_ref)
     half = out_ref.shape[2]
     mass = total[:, half:]
     duals_ref[...] = TAU * (jnp.log(cluster_mass_ref[...]) - jnp.log(mass))
@@ -341,31 +348,38 @@
         out_specs=[vmem, vmem],
         out_shape=[
             pltpu.VMEM((NX * NZ, rows, half), jnp.bfloat16),
-            jax.ShapeDtypeStruct(cluster_mass.shape, jnp.float32),
+            pltpu.VMEM(cluster_mass.shape, jnp.float32),
         ],
         compiler_params=pltpu.CompilerParams(vmem_limit_bytes=8 * MIB),
         name="finish",
     )(place, got, cluster_mass)
 
 
-def join_kernel(core_ref, block_ref, other_ref, out_ref):
-    half = block_ref.shape[1]
-    core = core_ref[0]
-    out_ref[:, pl.ds(pl.multiple_of(core * half, half), half)] = block_ref[...]
-    out_ref[:, pl.ds(pl.multiple_of((1 - core) * half, half), half)] = other_ref[...]
-
-
-def join_call(core, block, other):
-    rows, half = block.shape
-    vmem = pl.BlockSpec(memory_space=pltpu.VMEM)
-    return pl.pallas_call(
-        join_kernel,
-        in_specs=[pl.BlockSpec(memory_space=pltpu.SMEM), vmem, vmem],
-        out_specs=vmem,
-        out_shape=jax.ShapeDtypeStruct((rows, 2 * half), jnp.bfloat16),
-        compiler_params=pltpu.CompilerParams(vmem_limit_bytes=8 * MIB),
-        name="join",
-    )(core, block, other)
+def write_kernel(core_ref, half_ref, *refs):
+    out_hbm, sem = refs[-2:]
+    half = half_ref.shape[1]
+    columns = pl.ds(pl.multiple_of(core_ref[0] * half, half), half)
+    copy = pltpu.make_async_copy(half_ref, out_hbm.at[:, columns], sem)
+    copy.start()
+    copy.wait()
+
+
+def write_call(core, half, out):
+    rows, width = half.shape
+    hbm = pl.BlockSpec(memory_space=pltpu.HBM)
+    specs = [pl.BlockSpec(memory_space=pltpu.SMEM), pl.BlockSpec(memory_space=pltpu.VMEM)]
+    operands = (core, half) if out is None else (core, half, out)
+    return pl.pallas_call(
+        write_kernel,
+        in_specs=specs + [hbm] * (len(operands) - 2),
+        out_specs=hbm,
+        out_shape=jax.ShapeDtypeStruct((rows, 2 * width), half.dtype),
+        scratch_shapes=[pltpu.SemaphoreType.DMA],
+        input_output_aliases={} if out is None else {2: 0},
+        compiler_params=pltpu.CompilerParams(vmem_limit_bytes=4 * MIB),
+        cost_estimate=pl.CostEstimate(flops=0, bytes_accessed=8 * rows * width, transcendentals=0),
+        name="write",
+    )(*operands)
 
 
 def sum_all(copies):
@@ -393,7 +407,9 @@
     packed = lax.all_to_all(packed, ("z",), 0, 0, tiled=True)
     mine, duals = finish_call(packed, cluster_mass, place)
     block = lax.all_to_all(mine, ("x", "z"), 0, 0, tiled=True).reshape(n_clusters // NY, half)
-    return join_call(core, block, swap_cores(block)), duals.reshape(n_clusters)
+    other = swap_cores(block)
+    out = write_call(core, block, None)
+    return write_call(1 - core, other, out), duals.reshape(n_clusters)
 
 
 def solution(mesh):

time: 126 us -> 124 us (0.984)
  blocking collectives: 97.5 us -> 95.7 us
    all_to_all x1, blocking collectives: 21.1 us -> 19.8 us  [per_device(): lax.all_to_all(packed, ('y', 'x'), 0, 0, tiled=True)]
  transfers between devices with their start and end apart: 3 -> 3, of which waited for: 1 -> 0; matrix products, arithmetic and copies ran while one was open for 0% -> 0% of each run, Pallas kernels for 2% -> 2%
where the time goes in v5:
time: 124 us
  blocking collectives  95.7 us (77%)
  Pallas kernels  21.3 us (17%)
  starting transfers between devices  5.12 us (4%)
    all_to_all x2, blocking collectives, sum_all(): return lax.all_to_all(sum_call(got, NZ * NC), ('z', 'c'), 0, 0, tiled=True)  29.5 us
    all_to_all x2, blocking collectives, sum_all(): got = lax.all_to_all(copies, ('x', 'y'), 0, 0, tiled=True)  23.1 us
    all_to_all x1, blocking collectives, per_device(): lax.all_to_all(packed, ('y', 'x'), 0, 0, tiled=True)  19.8 us
    all_to_all x1, blocking collectives, per_device(): lax.all_to_all(mine, ('x', 'z'), 0, 0, tiled=True)  12.6 us
    all_to_all x1, blocking collectives, per_device(): packed = lax.all_to_all(packed, ('z',), 0, 0, tiled=True)  10.7 us
    pallas_call x1, Pallas kernels, first_call(): pl.pallas_call(functools.partial(first_kernel, loga), in_specs=[pl.BlockS...  8.55 us
    ppermute x3, starting transfers between devices, swap_cores(): return lax.ppermute(value, 'c', [(0, 1), (1, 0)])  5.12 us
    pallas_call x1, Pallas kernels, last_call(): pl.pallas_call(functools.partial(last_kernel, loga), in_specs=[pl.BlockSp...  4.99 us
  transfers between devices with their start and end apart: 3, of which 0 were waited for; matrix products, arithmetic and copies ran while one was open for 0% of the time, Pallas kernels for 2%

profile of v5, /device:TPU:1, one launch (start us, length us, event | category | flops | bytes accessed | tf_op | source)
XLA Modules:
  0.0 123.6 jit_solution(1439224718817895007)
XLA Ops:
  0.6 0.0 copy-start
  0.7 8.5 %first.1 = (f32[4,1024,512]{2,1,0:T(8,128)S(1)}, bf16[16,8,128]{2,1,0:T(8,128)(2,1)S(1)}, bf16[2048,1024]{1,0:T(8,128)(2,1)S(1)}) custom-call(bf16[2048,1024]{1,0:T(8,128)(2,1)} %docs_hbm, bf16[1024,1024]{1,0:T(8,128)(2,1)} %cent_hbm.1), custom_call_target="tpu_custom_call" | custom-call | tf_op jit(solution)/shard_map/first/pallas_call | solution.py:121
  9.2 13.8 %all_to_all.35.got_ref = bf16[16,8,128]{2,1,0:T(8,128)(2,1)S(1)} all-to-all(bf16[16,8,128]{2,1,0:T(8,128)(2,1)S(1)} %get-tuple-element.17), channel_id=1, replica_groups=mesh['x'=4,'z'=8,'c'=2,'y'=4] {'x','y'}, dimensions={0} | all-to-all | bytes 65536 | tf_op jit(solution)/shard_map/all_to_all | solution.py:386
  23.1 17.8 %all_to_all.36.got_ref = bf16[16,8,128]{2,1,0:T(8,128)(2,1)S(1)} all-to-all(bf16[16,8,128]{2,1,0:T(8,128)(2,1)S(1)} %sum.2), channel_id=1, replica_groups=mesh['x'=4,'z'=8,'c'=2,'y'=4] {'z','c'}, dimensions={0} | all-to-all | bytes 65536 | tf_op jit(solution)/shard_map/all_to_all | solution.py:387
  40.8 0.0 copy-done
  40.8 3.4 %middle.1 = bf16[16,8,128]{2,1,0:T(8,128)(2,1)S(1)} custom-call(f32[4,1024,512]{2,1,0:T(8,128)S(1)} %get-tuple-element.16.scores_ref, bf16[16,8,128]{2,1,0:T(8,128)(2,1)S(1)} %all_to_all.36.got_ref, f32[8,128]{1,0:T(8,128)S(1)} %bitcast.8), custom_call_target="tpu_custom_call" | custom-call | tf_op jit(solution)/shard_map/middle/pallas_call | solution.py:154
  44.3 9.3 %all_to_all.37.got_ref = bf16[16,8,128]{2,1,0:T(8,128)(2,1)S(1)} all-to-all(bf16[16,8,128]{2,1,0:T(8,128)(2,1)S(1)} %middle.1), channel_id=1, replica_groups=mesh['x'=4,'z'=8,'c'=2,'y'=4] {'x','y'}, dimensions={0} | all-to-all | bytes 65536 | tf_op jit(solution)/shard_map/all_to_all | solution.py:386
  53.6 11.7 %all_to_all.38.got_ref = bf16[16,8,128]{2,1,0:T(8,128)(2,1)S(1)} all-to-all(bf16[16,8,128]{2,1,0:T(8,128)(2,1)S(1)} %sum.3), channel_id=1, replica_groups=mesh['x'=4,'z'=8,'c'=2,'y'=4] {'z','c'}, dimensions={0} | all-to-all | bytes 65536 | tf_op jit(solution)/shard_map/all_to_all | solution.py:387
  65.3 5.0 %last.1 = (bf16[1024,512]{1,0:T(8,128)(2,1)S(1)}, bf16[1024,2048]{1,0:T(8,128)(2,1)S(1)}, f32[1,8,128]{2,1,0:T(8,128)S(1)}) custom-call(s32[1]{0:T(128)} %bitcast.core_ref, f32[4,1024,512]{2,1,0:T(8,128)S(1)} %get-tuple-element.16.scores_ref, bf16[16,8,128]{2,1,0:T(8,128)(2,1)S(1)} %all_to_all.38.got_ref, f32[8,128]{1,0:T(8,128)S(1)} %bitcast.9, ...), custom_call_target="tpu_custom_call" | custom-call | tf_op jit(solution)/shard_map/last/pallas_call | solution.py:204
  70.3 0.7 collective-permute-start
  71.0 0.1 collective-permute-start.1
  71.1 2.3 %own.1.own_ref = f32[1024,512]{1,0:T(8,128)S(1)} custom-call(s32[1]{0:T(128)} %bitcast.core_ref, bf16[1024,2048]{1,0:T(8,128)(2,1)S(1)} %get-tuple-element.19.plan_ref, bf16[2048,1024]{1,0:T(8,128)(2,1)S(1)} %get-tuple-element.18.docs_ref), custom_call_target="tpu_custom_call" | custom-call | flops 2147483648 | bytes 6291456 | tf_op jit(solution)/shard_map/own/pallas_call | solution.py:237
  73.4 0.0 collective-permute-done.1.mass_got_ref
  73.4 0.0 collective-permute-done.got_ref
  73.4 0.2 pack.1
  73.7 19.8 %all_to_all.39.got_ref = bf16[16,272,128]{2,1,0:T(8,128)(2,1)S(1)} all-to-all(bf16[16,272,128]{2,1,0:T(8,128)(2,1)S(1)} %pack.1), channel_id=1, replica_groups=mesh['x'=4,'z'=8,'c'=2,'y'=4] {'y','x'}, dimensions={0} | all-to-all | bytes 2228224 | tf_op jit(solution)/shard_map/all_to_all | solution.py:406
  93.5 0.2 repack.1
  93.6 10.7 %all_to_all.40.got_ref = f32[8,8,640]{2,1,0:T(8,128)S(1)} all-to-all(f32[8,8,640]{2,1,0:T(8,128)S(1)} %repack.1), channel_id=1, replica_groups=mesh['x'=4,'z'=8,'c'=2,'y'=4] {'z'}, dimensions={0} | all-to-all | bytes 327680 | tf_op jit(solution)/shard_map/all_to_all | solution.py:407
  104.3 0.1 finish.1
  104.5 12.6 %all_to_all.41 = bf16[32,8,512]{2,1,0:T(8,128)(2,1)S(1)} all-to-all(bf16[32,8,512]{2,1,0:T(8,128)(2,1)S(1)} %get-tuple-element.22), channel_id=1, replica_groups=mesh['x'=4,'z'=8,'c'=2,'y'=4] {'x','z'}, dimensions={0} | all-to-all | bytes 524288 | tf_op jit(solution)/shard_map/all_to_all | solution.py:409
  117.1 4.3 %collective-permute-start.2 = (bf16[256,512]{1,0:T(8,128)(2,1)S(1)}, bf16[256,512]{1,0:T(8,128)(2,1)S(1)}, u32[]{:S(2)}, u32[]{:S(2)}) collective-permute-start(bf16[256,512]{1,0:T(8,128)(2,1)S(1)} %bitcast.6), channel_id=1, source_target_pairs={{0,4},{4,0},{1,5},{5,1},{2,6},{6,2},{3,7},{7,3},{8,12},{12,8},{9,1... | collective-permute-start | bytes 786440 | tf_op jit(solution)/shard_map/ppermute | solution.py:26
  121.4 0.6 copy.7
  122.0 0.7 write.2.refs_0_
  122.7 0.0 collective-permute-done.2.half_ref
  122.8 0.7 write.3
  (2 shorter events, 0.0 us)
Async XLA Ops:
  0.6 40.2 %copy-start = (f32[1024]{0:T(1024)S(1)}, f32[1024]{0:T(1024)}, u32[]{:S(2)}) copy-start(f32[1024]{0:T(1024)} %param.5) | copy-start | bytes 12292
  70.3 3.1 %collective-permute-start = (bf16[1024,512]{1,0:T(8,128)(2,1)S(1)}, bf16[1024,512]{1,0:T(8,128)(2,1)S(1)}, u32[]{:S(2)}, u32[]{:S(2)}) collective-permute-start(bf16[1024,512]{1,0:T(8,128)(2,1)S(1)} %get-tuple-element.20), channel_id=1, source_target_pairs={{0,4},{4,0},{1,5},{5,1},{2,6},{6,2},{3,7},{7,3},{8,12},{12,8},{9,1... | collective-permute-start | bytes 3145736 | tf_op jit(solution)/shard_map/ppermute | solution.py:26
  71.0 2.4 %collective-permute-start.1 = (f32[1,8,128]{2,1,0:T(8,128)S(1)}, f32[1,8,128]{2,1,0:T(8,128)S(1)}, u32[]{:S(2)}, u32[]{:S(2)}) collective-permute-start(f32[1,8,128]{2,1,0:T(8,128)S(1)} %get-tuple-element.21.mass_ref), channel_id=1, source_target_pairs={{0,4},{4,0},{1,5},{5,1},{2,6},{6,2},{3,7},{7,3},{8,12},{12,8},{9,1... | collective-permute-start | bytes 12296 | tf_op jit(solution)/shard_map/ppermute | solution.py:26
  117.1 5.7 %collective-permute-start.2 = (bf16[256,512]{1,0:T(8,128)(2,1)S(1)}, bf16[256,512]{1,0:T(8,128)(2,1)S(1)}, u32[]{:S(2)}, u32[]{:S(2)}) collective-permute-start(bf16[256,512]{1,0:T(8,128)(2,1)S(1)} %bitcast.6), channel_id=1, source_target_pairs={{0,4},{4,0},{1,5},{5,1},{2,6},{6,2},{3,7},{7,3},{8,12},{12,8},{9,1... | collective-permute-start | bytes 786440 | tf_op jit(solution)/shard_map/ppermute | solution.py:26

commit v6 on v5

--- a/solution.py
+++ b/solution.py
@@ -297,15 +297,19 @@
 
 
 def repack_kernel(slab, got_ref, out_ref):
-    groups = out_ref.shape[2] // LANES - 1
+    groups = out_ref.shape[2] // LANES - 2
     rows = slab // NZ
     total = sum_slots(got_ref)
     mass = total[groups * slab : groups * slab + 8] + total[groups * slab + 8 :]
+    high = mass.astype(jnp.bfloat16)
+    low = (mass - high.astype(jnp.float32)).astype(jnp.bfloat16)
+    total = total.astype(jnp.bfloat16)
     for k in range(NZ):
         for group in range(groups):
             first = group * slab + k * rows
             out_ref[k, :, group * LANES : (group + 1) * LANES] = total[first : first + rows]
-        out_ref[k, :, groups * LANES :] = mass
+        out_ref[k, :, groups * LANES : (groups + 1) * LANES] = high
+        out_ref[k, :, (groups + 1) * LANES :] = low
 
 
 def repack_call(got, slab):
@@ -315,7 +319,7 @@
         functools.partial(repack_kernel, slab),
         in_specs=[vmem],
         out_specs=vmem,
-        out_shape=pltpu.VMEM((NZ, slab // NZ, (groups + 1) * LANES), jnp.float32),
+        out_shape=pltpu.VMEM((NZ, slab // NZ, (groups + 2) * LANES), jnp.bfloat16),
         compiler_params=pltpu.CompilerParams(vmem_limit_bytes=8 * MIB),
         name="repack",
     )(got)
@@ -324,7 +328,7 @@
 def finish_kernel(place_ref, got_ref, cluster_mass_ref, out_ref, duals_ref):
     total = sum_slots(got_ref)
     half = out_ref.shape[2]
-    mass = total[:, half:]
+    mass = total[:, half : half + LANES] + total[:, half + LANES :]
     duals_ref[...] = TAU * (jnp.log(cluster_mass_ref[...]) - jnp.log(mass))
     place = place_ref[0]
     group = place // LANES
@@ -340,7 +344,7 @@
 
 
 def finish_call(got, cluster_mass, place):
-    rows, half = got.shape[1], got.shape[2] - LANES
+    rows, half = got.shape[1], got.shape[2] - 2 * LANES
     vmem = pl.BlockSpec(memory_space=pltpu.VMEM)
     return pl.pallas_call(
         finish_kernel,

time: 124 us -> 123 us (level)
  no operation moved by 1% of the time
where the time goes in v6:
time: 123 us
  blocking collectives  95.1 us (77%)
  Pallas kernels  21.3 us (17%)
  starting transfers between devices  5.07 us (4%)
    all_to_all x2, blocking collectives, sum_all(): return lax.all_to_all(sum_call(got, NZ * NC), ('z', 'c'), 0, 0, tiled=True)  29.5 us
    all_to_all x2, blocking collectives, sum_all(): got = lax.all_to_all(copies, ('x', 'y'), 0, 0, tiled=True)  23.1 us
    all_to_all x1, blocking collectives, per_device(): lax.all_to_all(packed, ('y', 'x'), 0, 0, tiled=True)  19.8 us
    all_to_all x1, blocking collectives, per_device(): lax.all_to_all(mine, ('x', 'z'), 0, 0, tiled=True)  12.6 us
    all_to_all x1, blocking collectives, per_device(): packed = lax.all_to_all(packed, ('z',), 0, 0, tiled=True)  10.1 us
    pallas_call x1, Pallas kernels, first_call(): pl.pallas_call(functools.partial(first_kernel, loga), in_specs=[pl.BlockS...  8.55 us
    ppermute x3, starting transfers between devices, swap_cores(): return lax.ppermute(value, 'c', [(0, 1), (1, 0)])  5.07 us
    pallas_call x1, Pallas kernels, last_call(): pl.pallas_call(functools.partial(last_kernel, loga), in_specs=[pl.BlockSp...  4.99 us
  transfers between devices with their start and end apart: 3, of which 0 were waited for; matrix products, arithmetic and copies ran while one was open for 0% of the time, Pallas kernels for 2%

profile of v6, /device:TPU:1, one launch (start us, length us, event | category | flops | bytes accessed | tf_op | source)
XLA Modules:
  0.0 122.9 jit_solution(9183358035170168461)
XLA Ops:
  0.6 0.0 copy-start
  0.7 8.5 %first.1 = (f32[4,1024,512]{2,1,0:T(8,128)S(1)}, bf16[16,8,128]{2,1,0:T(8,128)(2,1)S(1)}, bf16[2048,1024]{1,0:T(8,128)(2,1)S(1)}) custom-call(bf16[2048,1024]{1,0:T(8,128)(2,1)} %docs_hbm, bf16[1024,1024]{1,0:T(8,128)(2,1)} %cent_hbm.1), custom_call_target="tpu_custom_call" | custom-call | tf_op jit(solution)/shard_map/first/pallas_call | solution.py:121
  9.2 13.8 %all_to_all.35.got_ref = bf16[16,8,128]{2,1,0:T(8,128)(2,1)S(1)} all-to-all(bf16[16,8,128]{2,1,0:T(8,128)(2,1)S(1)} %get-tuple-element.17), channel_id=1, replica_groups=mesh['x'=4,'z'=8,'c'=2,'y'=4] {'x','y'}, dimensions={0} | all-to-all | bytes 65536 | tf_op jit(solution)/shard_map/all_to_all | solution.py:390
  23.1 17.8 %all_to_all.36.got_ref = bf16[16,8,128]{2,1,0:T(8,128)(2,1)S(1)} all-to-all(bf16[16,8,128]{2,1,0:T(8,128)(2,1)S(1)} %sum.2), channel_id=1, replica_groups=mesh['x'=4,'z'=8,'c'=2,'y'=4] {'z','c'}, dimensions={0} | all-to-all | bytes 65536 | tf_op jit(solution)/shard_map/all_to_all | solution.py:391
  40.8 0.0 copy-done
  40.8 3.4 %middle.1 = bf16[16,8,128]{2,1,0:T(8,128)(2,1)S(1)} custom-call(f32[4,1024,512]{2,1,0:T(8,128)S(1)} %get-tuple-element.16.scores_ref, bf16[16,8,128]{2,1,0:T(8,128)(2,1)S(1)} %all_to_all.36.got_ref, f32[8,128]{1,0:T(8,128)S(1)} %bitcast.8), custom_call_target="tpu_custom_call" | custom-call | tf_op jit(solution)/shard_map/middle/pallas_call | solution.py:154
  44.3 9.3 %all_to_all.37.got_ref = bf16[16,8,128]{2,1,0:T(8,128)(2,1)S(1)} all-to-all(bf16[16,8,128]{2,1,0:T(8,128)(2,1)S(1)} %middle.1), channel_id=1, replica_groups=mesh['x'=4,'z'=8,'c'=2,'y'=4] {'x','y'}, dimensions={0} | all-to-all | bytes 65536 | tf_op jit(solution)/shard_map/all_to_all | solution.py:390
  53.6 11.7 %all_to_all.38.got_ref = bf16[16,8,128]{2,1,0:T(8,128)(2,1)S(1)} all-to-all(bf16[16,8,128]{2,1,0:T(8,128)(2,1)S(1)} %sum.3), channel_id=1, replica_groups=mesh['x'=4,'z'=8,'c'=2,'y'=4] {'z','c'}, dimensions={0} | all-to-all | bytes 65536 | tf_op jit(solution)/shard_map/all_to_all | solution.py:391
  65.3 5.0 %last.1 = (bf16[1024,512]{1,0:T(8,128)(2,1)S(1)}, bf16[1024,2048]{1,0:T(8,128)(2,1)S(1)}, f32[1,8,128]{2,1,0:T(8,128)S(1)}) custom-call(s32[1]{0:T(128)} %bitcast.core_ref, f32[4,1024,512]{2,1,0:T(8,128)S(1)} %get-tuple-element.16.scores_ref, bf16[16,8,128]{2,1,0:T(8,128)(2,1)S(1)} %all_to_all.38.got_ref, f32[8,128]{1,0:T(8,128)S(1)} %bitcast.9, ...), custom_call_target="tpu_custom_call" | custom-call | tf_op jit(solution)/shard_map/last/pallas_call | solution.py:204
  70.3 0.7 collective-permute-start
  71.0 0.1 collective-permute-start.1
  71.1 2.3 %own.1.own_ref = f32[1024,512]{1,0:T(8,128)S(1)} custom-call(s32[1]{0:T(128)} %bitcast.core_ref, bf16[1024,2048]{1,0:T(8,128)(2,1)S(1)} %get-tuple-element.19.plan_ref, bf16[2048,1024]{1,0:T(8,128)(2,1)S(1)} %get-tuple-element.18.docs_ref), custom_call_target="tpu_custom_call" | custom-call | flops 2147483648 | bytes 6291456 | tf_op jit(solution)/shard_map/own/pallas_call | solution.py:237
  73.4 0.0 collective-permute-done.1.mass_got_ref
  73.4 0.0 collective-permute-done.got_ref
  73.4 0.2 pack.1
  73.7 19.8 %all_to_all.39.got_ref = bf16[16,272,128]{2,1,0:T(8,128)(2,1)S(1)} all-to-all(bf16[16,272,128]{2,1,0:T(8,128)(2,1)S(1)} %pack.1), channel_id=1, replica_groups=mesh['x'=4,'z'=8,'c'=2,'y'=4] {'y','x'}, dimensions={0} | all-to-all | bytes 2228224 | tf_op jit(solution)/shard_map/all_to_all | solution.py:410
  93.5 0.2 repack.1
  93.6 10.1 %all_to_all.40.got_ref = bf16[8,8,768]{2,1,0:T(8,128)(2,1)S(1)} all-to-all(bf16[8,8,768]{2,1,0:T(8,128)(2,1)S(1)} %repack.1), channel_id=1, replica_groups=mesh['x'=4,'z'=8,'c'=2,'y'=4] {'z'}, dimensions={0} | all-to-all | bytes 196608 | tf_op jit(solution)/shard_map/all_to_all | solution.py:411
  103.7 0.1 finish.1
  103.8 12.6 %all_to_all.41 = bf16[32,8,512]{2,1,0:T(8,128)(2,1)S(1)} all-to-all(bf16[32,8,512]{2,1,0:T(8,128)(2,1)S(1)} %get-tuple-element.22), channel_id=1, replica_groups=mesh['x'=4,'z'=8,'c'=2,'y'=4] {'x','z'}, dimensions={0} | all-to-all | bytes 524288 | tf_op jit(solution)/shard_map/all_to_all | solution.py:413
  116.4 4.3 %collective-permute-start.2 = (bf16[256,512]{1,0:T(8,128)(2,1)S(1)}, bf16[256,512]{1,0:T(8,128)(2,1)S(1)}, u32[]{:S(2)}, u32[]{:S(2)}) collective-permute-start(bf16[256,512]{1,0:T(8,128)(2,1)S(1)} %bitcast.6), channel_id=1, source_target_pairs={{0,4},{4,0},{1,5},{5,1},{2,6},{6,2},{3,7},{7,3},{8,12},{12,8},{9,1... | collective-permute-start | bytes 786440 | tf_op jit(solution)/shard_map/ppermute | solution.py:26
  120.7 0.6 copy.7
  121.3 0.7 write.2.refs_0_
  122.0 0.0 collective-permute-done.2.half_ref
  122.1 0.7 write.3
  (2 shorter events, 0.0 us)
Async XLA Ops:
  0.6 40.2 %copy-start = (f32[1024]{0:T(1024)S(1)}, f32[1024]{0:T(1024)}, u32[]{:S(2)}) copy-start(f32[1024]{0:T(1024)} %param.5) | copy-start | bytes 12292
  70.3 3.1 %collective-permute-start = (bf16[1024,512]{1,0:T(8,128)(2,1)S(1)}, bf16[1024,512]{1,0:T(8,128)(2,1)S(1)}, u32[]{:S(2)}, u32[]{:S(2)}) collective-permute-start(bf16[1024,512]{1,0:T(8,128)(2,1)S(1)} %get-tuple-element.20), channel_id=1, source_target_pairs={{0,4},{4,0},{1,5},{5,1},{2,6},{6,2},{3,7},{7,3},{8,12},{12,8},{9,1... | collective-permute-start | bytes 3145736 | tf_op jit(solution)/shard_map/ppermute | solution.py:26
  71.0 2.4 %collective-permute-start.1 = (f32[1,8,128]{2,1,0:T(8,128)S(1)}, f32[1,8,128]{2,1,0:T(8,128)S(1)}, u32[]{:S(2)}, u32[]{:S(2)}) collective-permute-start(f32[1,8,128]{2,1,0:T(8,128)S(1)} %get-tuple-element.21.mass_ref), channel_id=1, source_target_pairs={{0,4},{4,0},{1,5},{5,1},{2,6},{6,2},{3,7},{7,3},{8,12},{12,8},{9,1... | collective-permute-start | bytes 12296 | tf_op jit(solution)/shard_map/ppermute | solution.py:26
  116.4 5.6 %collective-permute-start.2 = (bf16[256,512]{1,0:T(8,128)(2,1)S(1)}, bf16[256,512]{1,0:T(8,128)(2,1)S(1)}, u32[]{:S(2)}, u32[]{:S(2)}) collective-permute-start(bf16[256,512]{1,0:T(8,128)(2,1)S(1)} %bitcast.6), channel_id=1, source_target_pairs={{0,4},{4,0},{1,5},{5,1},{2,6},{6,2},{3,7},{7,3},{8,12},{12,8},{9,1... | collective-permute-start | bytes 786440 | tf_op jit(solution)/shard_map/ppermute | solution.py:26

commit v7 on v6

--- a/solution.py
+++ b/solution.py
@@ -16,7 +16,6 @@
 AXES = ("x", "z", "c", "y")
 LANES = 128
 BLOCK = 512
-GROUP = 2
 CHUNK = 64
 LOG2E = 1 / math.log(2)
 MIB = 2**20
@@ -89,27 +88,31 @@
     for block in range(n_blocks):
         rows = pl.ds(block * BLOCK, BLOCK)
         copies.append(pltpu.make_async_copy(docs_hbm.at[rows], docs_ref.at[rows], sems.at[block]))
-    for copy in copies[: 1 + GROUP]:
+    for copy in copies[:2]:
         copy.start()
     acc[...] = jnp.zeros_like(acc)
     copies[0].wait()
-    for block in range(n_blocks + 1):
-        if block % GROUP == 0 and block < n_blocks:
-            for k in range(block, block + GROUP):
-                copies[k + 1].wait()
-            if block == 0:
-                for copy in copies[1 + GROUP :]:
-                    copy.start()
-            scores = lax.dot_general(
-                cent_ref[...],
-                docs_ref[block * BLOCK : (block + GROUP) * BLOCK, :],
-                (((1,), (1,)), ((), ())),
-                preferred_element_type=jnp.float32,
-            ) * (TEMP / math.sqrt(D) * LOG2E)
-            for k in range(GROUP):
-                scores_ref[block + k] = scores[:, k * BLOCK : (k + 1) * BLOCK]
-        if block > 0:
-            block_masses(scores_ref.at[block - 1], slice(0, BLOCK), None, loga, functools.partial(add_lanes, acc))
+    start, ready = 0, []
+    for group in (1, n_blocks - 1):
+        blocks = range(start, start + group)
+        for block in blocks:
+            copies[block + 1].wait()
+        if start == 0:
+            for copy in copies[2:]:
+                copy.start()
+        scores = lax.dot_general(
+            cent_ref[...],
+            docs_ref[start * BLOCK : (start + group) * BLOCK, :],
+            (((1,), (1,)), ((), ())),
+            preferred_element_type=jnp.float32,
+        ) * (TEMP / math.sqrt(D) * LOG2E)
+        for k, block in enumerate(blocks):
+            scores_ref[block] = scores[:, k * BLOCK : (k + 1) * BLOCK]
+        for block in ready:
+            block_masses(scores_ref.at[block], slice(0, BLOCK), None, loga, functools.partial(add_lanes, acc))
+        start, ready = start + group, blocks
+    for block in ready:
+        block_masses(scores_ref.at[block], slice(0, BLOCK), None, loga, functools.partial(add_lanes, acc))
     column_sums(acc, mass_ref)
 
 

time: 123 us -> 123 us (level)
  no operation moved by 1% of the time
where the time goes in v7:
time: 123 us
  blocking collectives  95.1 us (77%)
  Pallas kernels  21.2 us (17%)
  starting transfers between devices  5.08 us (4%)
    all_to_all x2, blocking collectives, sum_all(): return lax.all_to_all(sum_call(got, NZ * NC), ('z', 'c'), 0, 0, tiled=True)  29.4 us
    all_to_all x2, blocking collectives, sum_all(): got = lax.all_to_all(copies, ('x', 'y'), 0, 0, tiled=True)  23.1 us
    all_to_all x1, blocking collectives, per_device(): lax.all_to_all(packed, ('y', 'x'), 0, 0, tiled=True)  19.8 us
    all_to_all x1, blocking collectives, per_device(): lax.all_to_all(mine, ('x', 'z'), 0, 0, tiled=True)  12.6 us
    all_to_all x1, blocking collectives, per_device(): packed = lax.all_to_all(packed, ('z',), 0, 0, tiled=True)  10.1 us
    pallas_call x1, Pallas kernels, first_call(): pl.pallas_call(functools.partial(first_kernel, loga), in_specs=[pl.BlockS...  8.48 us
    ppermute x3, starting transfers between devices, swap_cores(): return lax.ppermute(value, 'c', [(0, 1), (1, 0)])  5.08 us
    pallas_call x1, Pallas kernels, last_call(): pl.pallas_call(functools.partial(last_kernel, loga), in_specs=[pl.BlockSp...  4.99 us
  transfers between devices with their start and end apart: 3, of which 0 were waited for; matrix products, arithmetic and copies ran while one was open for 0% of the time, Pallas kernels for 2%

profile of v7, /device:TPU:1, one launch (start us, length us, event | category | flops | bytes accessed | tf_op | source)
XLA Modules:
  0.0 122.9 jit_solution(3969210368623373444)
XLA Ops:
  0.6 0.0 copy-start
  0.7 8.5 %first.1 = (f32[4,1024,512]{2,1,0:T(8,128)S(1)}, bf16[16,8,128]{2,1,0:T(8,128)(2,1)S(1)}, bf16[2048,1024]{1,0:T(8,128)(2,1)S(1)}) custom-call(bf16[2048,1024]{1,0:T(8,128)(2,1)} %docs_hbm, bf16[1024,1024]{1,0:T(8,128)(2,1)} %cent_hbm.1), custom_call_target="tpu_custom_call" | custom-call | tf_op jit(solution)/shard_map/first/pallas_call | solution.py:124
  9.1 13.8 %all_to_all.35.got_ref = bf16[16,8,128]{2,1,0:T(8,128)(2,1)S(1)} all-to-all(bf16[16,8,128]{2,1,0:T(8,128)(2,1)S(1)} %get-tuple-element.17), channel_id=1, replica_groups=mesh['x'=4,'z'=8,'c'=2,'y'=4] {'x','y'}, dimensions={0} | all-to-all | bytes 65536 | tf_op jit(solution)/shard_map/all_to_all | solution.py:393
  23.0 17.8 %all_to_all.36.got_ref = bf16[16,8,128]{2,1,0:T(8,128)(2,1)S(1)} all-to-all(bf16[16,8,128]{2,1,0:T(8,128)(2,1)S(1)} %sum.2), channel_id=1, replica_groups=mesh['x'=4,'z'=8,'c'=2,'y'=4] {'z','c'}, dimensions={0} | all-to-all | bytes 65536 | tf_op jit(solution)/shard_map/all_to_all | solution.py:394
  40.8 0.0 copy-done
  40.8 3.4 %middle.1 = bf16[16,8,128]{2,1,0:T(8,128)(2,1)S(1)} custom-call(f32[4,1024,512]{2,1,0:T(8,128)S(1)} %get-tuple-element.16.scores_ref, bf16[16,8,128]{2,1,0:T(8,128)(2,1)S(1)} %all_to_all.36.got_ref, f32[8,128]{1,0:T(8,128)S(1)} %bitcast.8), custom_call_target="tpu_custom_call" | custom-call | tf_op jit(solution)/shard_map/middle/pallas_call | solution.py:157
  44.2 9.3 %all_to_all.37.got_ref = bf16[16,8,128]{2,1,0:T(8,128)(2,1)S(1)} all-to-all(bf16[16,8,128]{2,1,0:T(8,128)(2,1)S(1)} %middle.1), channel_id=1, replica_groups=mesh['x'=4,'z'=8,'c'=2,'y'=4] {'x','y'}, dimensions={0} | all-to-all | bytes 65536 | tf_op jit(solution)/shard_map/all_to_all | solution.py:393
  53.5 11.7 %all_to_all.38.got_ref = bf16[16,8,128]{2,1,0:T(8,128)(2,1)S(1)} all-to-all(bf16[16,8,128]{2,1,0:T(8,128)(2,1)S(1)} %sum.3), channel_id=1, replica_groups=mesh['x'=4,'z'=8,'c'=2,'y'=4] {'z','c'}, dimensions={0} | all-to-all | bytes 65536 | tf_op jit(solution)/shard_map/all_to_all | solution.py:394
  65.2 5.0 %last.1 = (bf16[1024,512]{1,0:T(8,128)(2,1)S(1)}, bf16[1024,2048]{1,0:T(8,128)(2,1)S(1)}, f32[1,8,128]{2,1,0:T(8,128)S(1)}) custom-call(s32[1]{0:T(128)} %bitcast.core_ref, f32[4,1024,512]{2,1,0:T(8,128)S(1)} %get-tuple-element.16.scores_ref, bf16[16,8,128]{2,1,0:T(8,128)(2,1)S(1)} %all_to_all.38.got_ref, f32[8,128]{1,0:T(8,128)S(1)} %bitcast.9, ...), custom_call_target="tpu_custom_call" | custom-call | tf_op jit(solution)/shard_map/last/pallas_call | solution.py:207
  70.2 0.7 collective-permute-start
  70.9 0.1 collective-permute-start.1
  71.0 2.3 %own.1.own_ref = f32[1024,512]{1,0:T(8,128)S(1)} custom-call(s32[1]{0:T(128)} %bitcast.core_ref, bf16[1024,2048]{1,0:T(8,128)(2,1)S(1)} %get-tuple-element.19.plan_ref, bf16[2048,1024]{1,0:T(8,128)(2,1)S(1)} %get-tuple-element.18.docs_ref), custom_call_target="tpu_custom_call" | custom-call | flops 2147483648 | bytes 6291456 | tf_op jit(solution)/shard_map/own/pallas_call | solution.py:240
  73.3 0.0 collective-permute-done.1.mass_got_ref
  73.3 0.0 collective-permute-done.got_ref
  73.3 0.2 pack.1
  73.6 19.8 %all_to_all.39.got_ref = bf16[16,272,128]{2,1,0:T(8,128)(2,1)S(1)} all-to-all(bf16[16,272,128]{2,1,0:T(8,128)(2,1)S(1)} %pack.1), channel_id=1, replica_groups=mesh['x'=4,'z'=8,'c'=2,'y'=4] {'y','x'}, dimensions={0} | all-to-all | bytes 2228224 | tf_op jit(solution)/shard_map/all_to_all | solution.py:413
  93.4 0.2 repack.1
  93.5 10.1 %all_to_all.40.got_ref = bf16[8,8,768]{2,1,0:T(8,128)(2,1)S(1)} all-to-all(bf16[8,8,768]{2,1,0:T(8,128)(2,1)S(1)} %repack.1), channel_id=1, replica_groups=mesh['x'=4,'z'=8,'c'=2,'y'=4] {'z'}, dimensions={0} | all-to-all | bytes 196608 | tf_op jit(solution)/shard_map/all_to_all | solution.py:414
  103.6 0.1 finish.1
  103.7 12.6 %all_to_all.41 = bf16[32,8,512]{2,1,0:T(8,128)(2,1)S(1)} all-to-all(bf16[32,8,512]{2,1,0:T(8,128)(2,1)S(1)} %get-tuple-element.22), channel_id=1, replica_groups=mesh['x'=4,'z'=8,'c'=2,'y'=4] {'x','z'}, dimensions={0} | all-to-all | bytes 524288 | tf_op jit(solution)/shard_map/all_to_all | solution.py:416
  116.4 4.3 %collective-permute-start.2 = (bf16[256,512]{1,0:T(8,128)(2,1)S(1)}, bf16[256,512]{1,0:T(8,128)(2,1)S(1)}, u32[]{:S(2)}, u32[]{:S(2)}) collective-permute-start(bf16[256,512]{1,0:T(8,128)(2,1)S(1)} %bitcast.6), channel_id=1, source_target_pairs={{0,4},{4,0},{1,5},{5,1},{2,6},{6,2},{3,7},{7,3},{8,12},{12,8},{9,1... | collective-permute-start | bytes 786440 | tf_op jit(solution)/shard_map/ppermute | solution.py:25
  120.7 0.6 copy.7
  121.2 0.7 write.2.refs_0_
  122.0 0.0 collective-permute-done.2.half_ref
  122.0 0.7 write.3
  (2 shorter events, 0.0 us)
Async XLA Ops:
  0.6 40.1 %copy-start = (f32[1024]{0:T(1024)S(1)}, f32[1024]{0:T(1024)}, u32[]{:S(2)}) copy-start(f32[1024]{0:T(1024)} %param.5) | copy-start | bytes 12292
  70.2 3.1 %collective-permute-start = (bf16[1024,512]{1,0:T(8,128)(2,1)S(1)}, bf16[1024,512]{1,0:T(8,128)(2,1)S(1)}, u32[]{:S(2)}, u32[]{:S(2)}) collective-permute-start(bf16[1024,512]{1,0:T(8,128)(2,1)S(1)} %get-tuple-element.20), channel_id=1, source_target_pairs={{0,4},{4,0},{1,5},{5,1},{2,6},{6,2},{3,7},{7,3},{8,12},{12,8},{9,1... | collective-permute-start | bytes 3145736 | tf_op jit(solution)/shard_map/ppermute | solution.py:25
  70.9 2.4 %collective-permute-start.1 = (f32[1,8,128]{2,1,0:T(8,128)S(1)}, f32[1,8,128]{2,1,0:T(8,128)S(1)}, u32[]{:S(2)}, u32[]{:S(2)}) collective-permute-start(f32[1,8,128]{2,1,0:T(8,128)S(1)} %get-tuple-element.21.mass_ref), channel_id=1, source_target_pairs={{0,4},{4,0},{1,5},{5,1},{2,6},{6,2},{3,7},{7,3},{8,12},{12,8},{9,1... | collective-permute-start | bytes 12296 | tf_op jit(solution)/shard_map/ppermute | solution.py:25
  116.4 5.6 %collective-permute-start.2 = (bf16[256,512]{1,0:T(8,128)(2,1)S(1)}, bf16[256,512]{1,0:T(8,128)(2,1)S(1)}, u32[]{:S(2)}, u32[]{:S(2)}) collective-permute-start(bf16[256,512]{1,0:T(8,128)(2,1)S(1)} %bitcast.6), channel_id=1, source_target_pairs={{0,4},{4,0},{1,5},{5,1},{2,6},{6,2},{3,7},{7,3},{8,12},{12,8},{9,1... | collective-permute-start | bytes 786440 | tf_op jit(solution)/shard_map/ppermute | solution.py:25

commit v8 on v6

--- a/solution.py
+++ b/solution.py
@@ -124,7 +124,7 @@
         out_specs=[vmem] * 3,
         out_shape=[
             pltpu.VMEM((n_blocks, n_clusters, BLOCK), jnp.float32),
-            pltpu.VMEM((NX * NY, n_clusters // LANES, LANES), jnp.bfloat16),
+            pltpu.VMEM((NZ * NC, n_clusters // LANES, LANES), jnp.bfloat16),
             pltpu.VMEM((n_docs, dim), jnp.bfloat16),
         ],
         scratch_shapes=[
@@ -155,7 +155,7 @@
         functools.partial(middle_kernel, loga),
         in_specs=[vmem] * 3,
         out_specs=vmem,
-        out_shape=pltpu.VMEM((NX * NY, n_clusters // LANES, LANES), jnp.bfloat16),
+        out_shape=pltpu.VMEM((NZ * NC, n_clusters // LANES, LANES), jnp.bfloat16),
         scratch_shapes=[
             pltpu.VMEM((n_clusters, LANES), jnp.float32),
             pltpu.VMEM((n_clusters, LANES), jnp.float32),
@@ -387,8 +387,8 @@
 
 
 def sum_all(copies):
-    got = lax.all_to_all(copies, ("x", "y"), 0, 0, tiled=True)
-    return lax.all_to_all(sum_call(got, NZ * NC), ("z", "c"), 0, 0, tiled=True)
+    got = lax.all_to_all(copies, ("z", "c"), 0, 0, tiled=True)
+    return lax.all_to_all(sum_call(got, NX * NY), ("x", "y"), 0, 0, tiled=True)
 
 
 def per_device(documents, centroids, cluster_mass):

time: 123 us -> 123 us (level)
  starting transfers between devices: 5.07 us -> 6.49 us
  blocking collectives: 95.1 us -> 93.7 us
    all_to_all x4, blocking collectives: 52.6 us -> 51.2 us  [the longest x2 28.9 us: sum_all(): got = lax.all_to_all(copies, ('z', 'c'), 0, 0, tiled=True)]
    ppermute x3, starting transfers between devices: 5.07 us -> 6.49 us  [swap_cores(): return lax.ppermute(value, 'c', [(0, 1), (1, 0)])]
where the time goes in v8:
time: 123 us
  blocking collectives  93.7 us (76%)
  Pallas kernels  21.3 us (17%)
  starting transfers between devices  6.49 us (5%)
    all_to_all x2, blocking collectives, sum_all(): got = lax.all_to_all(copies, ('z', 'c'), 0, 0, tiled=True)  28.9 us
    all_to_all x2, blocking collectives, sum_all(): return lax.all_to_all(sum_call(got, NX * NY), ('x', 'y'), 0, 0, tiled=True)  22.3 us
    all_to_all x1, blocking collectives, per_device(): lax.all_to_all(packed, ('y', 'x'), 0, 0, tiled=True)  19.8 us
    all_to_all x1, blocking collectives, per_device(): lax.all_to_all(mine, ('x', 'z'), 0, 0, tiled=True)  12.6 us
    all_to_all x1, blocking collectives, per_device(): packed = lax.all_to_all(packed, ('z',), 0, 0, tiled=True)  10.1 us
    pallas_call x1, Pallas kernels, first_call(): pl.pallas_call(functools.partial(first_kernel, loga), in_specs=[pl.BlockS...  8.55 us
    ppermute x3, starting transfers between devices, swap_cores(): return lax.ppermute(value, 'c', [(0, 1), (1, 0)])  6.49 us
    pallas_call x1, Pallas kernels, last_call(): pl.pallas_call(functools.partial(last_kernel, loga), in_specs=[pl.BlockSp...  4.99 us
  transfers between devices with their start and end apart: 3, of which 0 were waited for; matrix products, arithmetic and copies ran while one was open for 0% of the time, Pallas kernels for 2%

profile of v8, /device:TPU:1, one launch (start us, length us, event | category | flops | bytes accessed | tf_op | source)
XLA Modules:
  0.0 122.9 jit_solution(12769141065907163527)
XLA Ops:
  0.6 0.0 copy-start
  0.7 8.5 %first.1 = (f32[4,1024,512]{2,1,0:T(8,128)S(1)}, bf16[16,8,128]{2,1,0:T(8,128)(2,1)S(1)}, bf16[2048,1024]{1,0:T(8,128)(2,1)S(1)}) custom-call(bf16[2048,1024]{1,0:T(8,128)(2,1)} %docs_hbm, bf16[1024,1024]{1,0:T(8,128)(2,1)} %cent_hbm.1), custom_call_target="tpu_custom_call" | custom-call | tf_op jit(solution)/shard_map/first/pallas_call | solution.py:121
  9.2 17.2 %all_to_all.35.got_ref = bf16[16,8,128]{2,1,0:T(8,128)(2,1)S(1)} all-to-all(bf16[16,8,128]{2,1,0:T(8,128)(2,1)S(1)} %get-tuple-element.17), channel_id=1, replica_groups=mesh['x'=4,'z'=8,'c'=2,'y'=4] {'z','c'}, dimensions={0} | all-to-all | bytes 65536 | tf_op jit(solution)/shard_map/all_to_all | solution.py:390
  26.4 13.0 %all_to_all.36.got_ref = bf16[16,8,128]{2,1,0:T(8,128)(2,1)S(1)} all-to-all(bf16[16,8,128]{2,1,0:T(8,128)(2,1)S(1)} %sum.2), channel_id=1, replica_groups=mesh['x'=4,'z'=8,'c'=2,'y'=4] {'x','y'}, dimensions={0} | all-to-all | bytes 65536 | tf_op jit(solution)/shard_map/all_to_all | solution.py:391
  39.4 0.0 copy-done
  39.4 3.4 %middle.1 = bf16[16,8,128]{2,1,0:T(8,128)(2,1)S(1)} custom-call(f32[4,1024,512]{2,1,0:T(8,128)S(1)} %get-tuple-element.16.scores_ref, bf16[16,8,128]{2,1,0:T(8,128)(2,1)S(1)} %all_to_all.36.got_ref, f32[8,128]{1,0:T(8,128)S(1)} %bitcast.8), custom_call_target="tpu_custom_call" | custom-call | tf_op jit(solution)/shard_map/middle/pallas_call | solution.py:154
  42.9 11.7 %all_to_all.37.got_ref = bf16[16,8,128]{2,1,0:T(8,128)(2,1)S(1)} all-to-all(bf16[16,8,128]{2,1,0:T(8,128)(2,1)S(1)} %middle.1), channel_id=1, replica_groups=mesh['x'=4,'z'=8,'c'=2,'y'=4] {'z','c'}, dimensions={0} | all-to-all | bytes 65536 | tf_op jit(solution)/shard_map/all_to_all | solution.py:390
  54.6 9.3 %all_to_all.38.got_ref = bf16[16,8,128]{2,1,0:T(8,128)(2,1)S(1)} all-to-all(bf16[16,8,128]{2,1,0:T(8,128)(2,1)S(1)} %sum.3), channel_id=1, replica_groups=mesh['x'=4,'z'=8,'c'=2,'y'=4] {'x','y'}, dimensions={0} | all-to-all | bytes 65536 | tf_op jit(solution)/shard_map/all_to_all | solution.py:391
  63.9 5.0 %last.1 = (bf16[1024,512]{1,0:T(8,128)(2,1)S(1)}, bf16[1024,2048]{1,0:T(8,128)(2,1)S(1)}, f32[1,8,128]{2,1,0:T(8,128)S(1)}) custom-call(s32[1]{0:T(128)} %bitcast.core_ref, f32[4,1024,512]{2,1,0:T(8,128)S(1)} %get-tuple-element.16.scores_ref, bf16[16,8,128]{2,1,0:T(8,128)(2,1)S(1)} %all_to_all.38.got_ref, f32[8,128]{1,0:T(8,128)S(1)} %bitcast.9, ...), custom_call_target="tpu_custom_call" | custom-call | tf_op jit(solution)/shard_map/last/pallas_call | solution.py:204
  68.9 2.1 %collective-permute-start = (bf16[1024,512]{1,0:T(8,128)(2,1)S(1)}, bf16[1024,512]{1,0:T(8,128)(2,1)S(1)}, u32[]{:S(2)}, u32[]{:S(2)}) collective-permute-start(bf16[1024,512]{1,0:T(8,128)(2,1)S(1)} %get-tuple-element.20), channel_id=1, source_target_pairs={{0,4},{4,0},{1,5},{5,1},{2,6},{6,2},{3,7},{7,3},{8,12},{12,8},{9,1... | collective-permute-start | bytes 3145736 | tf_op jit(solution)/shard_map/ppermute | solution.py:26
  71.0 0.1 collective-permute-start.1
  71.1 2.3 %own.1.own_ref = f32[1024,512]{1,0:T(8,128)S(1)} custom-call(s32[1]{0:T(128)} %bitcast.core_ref, bf16[1024,2048]{1,0:T(8,128)(2,1)S(1)} %get-tuple-element.19.plan_ref, bf16[2048,1024]{1,0:T(8,128)(2,1)S(1)} %get-tuple-element.18.docs_ref), custom_call_target="tpu_custom_call" | custom-call | flops 2147483648 | bytes 6291456 | tf_op jit(solution)/shard_map/own/pallas_call | solution.py:237
  73.4 0.0 collective-permute-done.1.mass_got_ref
  73.4 0.0 collective-permute-done.got_ref
  73.4 0.2 pack.1
  73.7 19.8 %all_to_all.39.got_ref = bf16[16,272,128]{2,1,0:T(8,128)(2,1)S(1)} all-to-all(bf16[16,272,128]{2,1,0:T(8,128)(2,1)S(1)} %pack.1), channel_id=1, replica_groups=mesh['x'=4,'z'=8,'c'=2,'y'=4] {'y','x'}, dimensions={0} | all-to-all | bytes 2228224 | tf_op jit(solution)/shard_map/all_to_all | solution.py:410
  93.5 0.2 repack.1
  93.6 10.1 %all_to_all.40.got_ref = bf16[8,8,768]{2,1,0:T(8,128)(2,1)S(1)} all-to-all(bf16[8,8,768]{2,1,0:T(8,128)(2,1)S(1)} %repack.1), channel_id=1, replica_groups=mesh['x'=4,'z'=8,'c'=2,'y'=4] {'z'}, dimensions={0} | all-to-all | bytes 196608 | tf_op jit(solution)/shard_map/all_to_all | solution.py:411
  103.7 0.1 finish.1
  103.8 12.6 %all_to_all.41 = bf16[32,8,512]{2,1,0:T(8,128)(2,1)S(1)} all-to-all(bf16[32,8,512]{2,1,0:T(8,128)(2,1)S(1)} %get-tuple-element.22), channel_id=1, replica_groups=mesh['x'=4,'z'=8,'c'=2,'y'=4] {'x','z'}, dimensions={0} | all-to-all | bytes 524288 | tf_op jit(solution)/shard_map/all_to_all | solution.py:413
  116.4 4.3 %collective-permute-start.2 = (bf16[256,512]{1,0:T(8,128)(2,1)S(1)}, bf16[256,512]{1,0:T(8,128)(2,1)S(1)}, u32[]{:S(2)}, u32[]{:S(2)}) collective-permute-start(bf16[256,512]{1,0:T(8,128)(2,1)S(1)} %bitcast.6), channel_id=1, source_target_pairs={{0,4},{4,0},{1,5},{5,1},{2,6},{6,2},{3,7},{7,3},{8,12},{12,8},{9,1... | collective-permute-start | bytes 786440 | tf_op jit(solution)/shard_map/ppermute | solution.py:26
  120.7 0.6 copy.7
  121.3 0.7 write.2.refs_0_
  122.0 0.0 collective-permute-done.2.half_ref
  122.1 0.7 write.3
  (2 shorter events, 0.0 us)
Async XLA Ops:
  0.6 38.8 %copy-start = (f32[1024]{0:T(1024)S(1)}, f32[1024]{0:T(1024)}, u32[]{:S(2)}) copy-start(f32[1024]{0:T(1024)} %param.5) | copy-start | bytes 12292
  68.9 4.5 %collective-permute-start = (bf16[1024,512]{1,0:T(8,128)(2,1)S(1)}, bf16[1024,512]{1,0:T(8,128)(2,1)S(1)}, u32[]{:S(2)}, u32[]{:S(2)}) collective-permute-start(bf16[1024,512]{1,0:T(8,128)(2,1)S(1)} %get-tuple-element.20), channel_id=1, source_target_pairs={{0,4},{4,0},{1,5},{5,1},{2,6},{6,2},{3,7},{7,3},{8,12},{12,8},{9,1... | collective-permute-start | bytes 3145736 | tf_op jit(solution)/shard_map/ppermute | solution.py:26
  71.0 2.4 %collective-permute-start.1 = (f32[1,8,128]{2,1,0:T(8,128)S(1)}, f32[1,8,128]{2,1,0:T(8,128)S(1)}, u32[]{:S(2)}, u32[]{:S(2)}) collective-permute-start(f32[1,8,128]{2,1,0:T(8,128)S(1)} %get-tuple-element.21.mass_ref), channel_id=1, source_target_pairs={{0,4},{4,0},{1,5},{5,1},{2,6},{6,2},{3,7},{7,3},{8,12},{12,8},{9,1... | collective-permute-start | bytes 12296 | tf_op jit(solution)/shard_map/ppermute | solution.py:26
  116.4 5.6 %collective-permute-start.2 = (bf16[256,512]{1,0:T(8,128)(2,1)S(1)}, bf16[256,512]{1,0:T(8,128)(2,1)S(1)}, u32[]{:S(2)}, u32[]{:S(2)}) collective-permute-start(bf16[256,512]{1,0:T(8,128)(2,1)S(1)} %bitcast.6), channel_id=1, source_target_pairs={{0,4},{4,0},{1,5},{5,1},{2,6},{6,2},{3,7},{7,3},{8,12},{12,8},{9,1... | collective-permute-start | bytes 786440 | tf_op jit(solution)/shard_map/ppermute | solution.py:26
